TPU v7x, 256 devices: a whole 4x4x8 slice. The times are simulated.
256 devices in a mesh: ctx: 8 (over z_lo, y), exp: 32 (over z_hi, x, core).
Axes of the slice: x: 4, y: 4, z: 8 (z_hi: 4, z_lo: 2; z = z_hi * 2 + z_lo), core: 2. Of those that a mesh axis runs over, the one named last changes fastest.
Arguments:
- tokens: bfloat16 [32, 1024, 2048], P('exp', 'ctx'), may hold values from -6 to 6
- queries: bfloat16 [32, 1024, 1024], P('exp', 'ctx'), may hold values from -60 to 60
- keys: bfloat16 [32, 1024, 1024], P('exp', 'ctx'), may hold values from -4 to 4
- values: bfloat16 [32, 1024, 1024], P('exp', 'ctx'), may hold values from -12 to 12
- out_proj: bfloat16 [1024, 2048], replicated, may hold values from -0.1875 to 0.1875
- mod_scale: float32 [32, 2048], P('exp'), may hold values from -2.5 to 2.5
- mod_shift: float32 [32, 2048], P('exp'), may hold values from -2.5 to 2.5
- expert_ids: int32 [32, 1024, 2], P('exp', 'ctx'), may hold values from 0 to 63, all different within a row; in each aligned block of 128 rows (0 to 127, 128 to 255, ..., all dimensions but the last counted through in order) at most 6 rows name the same one
- gates: float32 [32, 1024, 2], P('exp', 'ctx'), may hold values from 0.2 to 1
- w_gate: bfloat16 [65536, 2048], P(('ctx', 'exp')), may hold values from -0.125 to 0.125
- w_up: bfloat16 [65536, 2048], P(('ctx', 'exp')), may hold values from -0.125 to 0.125
- w_down: bfloat16 [65536, 2048], P(('ctx', 'exp')), may hold values from -0.1875 to 0.1875
- out_grad: bfloat16 [32, 1024, 2048], P('exp', 'ctx'), may hold values from -0.1875 to 0.1875
Outputs:
- layer_out: bfloat16 [32, 1024, 2048], P('exp', 'ctx')
- grad_gate: bfloat16 [65536, 2048], P(('ctx', 'exp'))
- grad_up: bfloat16 [65536, 2048], P(('ctx', 'exp'))
- grad_down: bfloat16 [65536, 2048], P(('ctx', 'exp'))
Inputs may be any that keep to these rules, and one draw needn't show every extreme that they name: `expert_ids`: the two ids of a token differ. Among the 128 tokens of one device no expert is named more than 6 times, and in some device some expert exactly 6 times.
All inputs are finite; a program needn't handle non-finite values.
Results may differ from a plain program's by a relative error of at most 0.0075.
Values may be sent and summed in bfloat16 or wider, within the bound.
A program may use at most 128 MiB of HBM per device.

v0:
```python
import jax
import jax.numpy as jnp
from jax import lax
from jax.sharding import PartitionSpec as P

HEADS = 8
HD = 128
SHARDS = 4


def per_device(
    tokens,
    queries,
    keys,
    values,
    out_proj,
    mod_scale,
    mod_shift,
    expert_ids,
    gates,
    w_gate,
    w_up,
    w_down,
    out_grad,
):
    ctx_count = lax.axis_size("ctx")
    exp_count = lax.axis_size("exp")
    local_tokens = tokens.shape[1]
    model_width = tokens.shape[2]
    score_scale = HD ** (-0.5)
    query_rows = queries[0]
    key_rows = keys[0]
    value_rows = values[0]
    query_heads = query_rows.reshape(local_tokens, HEADS, HD)
    running_top = jnp.full((HEADS, local_tokens), -1e30, jnp.float32)
    key_piece = lax.all_gather(key_rows, "ctx", axis=0, tiled=True).reshape(-1, HEADS, HD)
    value_piece = lax.all_gather(value_rows, "ctx", axis=0, tiled=True).reshape(-1, HEADS, HD)
    scores = (
        jnp.einsum("qhd,khd->hqk", query_heads, key_piece, preferred_element_type=jnp.float32)
        * score_scale
    )
    new_top = jnp.maximum(running_top, jnp.max(scores, axis=-1))
    exponent = jnp.exp(scores - new_top[..., None])
    running_sum = jnp.sum(exponent, axis=-1)
    accum = jnp.einsum(
        "hqk,khd->hqd",
        exponent.astype(jnp.bfloat16),
        value_piece,
        preferred_element_type=jnp.float32,
    )
    attended = (
        jnp.transpose(accum / running_sum[..., None], (1, 0, 2))
        .reshape(local_tokens, HEADS * HD)
        .astype(jnp.bfloat16)
    )
    mixed = tokens[0].astype(jnp.float32) + jnp.dot(
        attended, out_proj, preferred_element_type=jnp.float32
    )
    mean_square = jnp.mean(mixed * mixed, axis=-1, keepdims=True)
    normed = (mixed * lax.rsqrt(mean_square + 1e-06) * (1.0 + mod_scale) + mod_shift).astype(
        jnp.bfloat16
    )
    expert_total = ctx_count * exp_count // SHARDS
    capacity = 3 * local_tokens // expert_total
    group_count = exp_count // SHARDS
    chosen = expert_ids[0].reshape(-1)
    one_hot = (chosen[:, None] == jnp.arange(expert_total, dtype=jnp.int32)[None, :]).astype(
        jnp.int32
    )
    before = jnp.cumsum(one_hot, axis=0) - one_hot
    slot_index = jnp.sum(one_hot * before, axis=1)
    position = chosen * capacity + slot_index
    chooser = (
        jnp.arange(expert_total * capacity, dtype=jnp.int32)[:, None] == position[None, :]
    ).astype(jnp.bfloat16)
    gate_flat = gates[0].reshape(-1)
    token_rows = jnp.repeat(normed, 2, axis=0)
    grad_rows = (
        gate_flat[:, None] * jnp.repeat(out_grad[0], 2, axis=0).astype(jnp.float32)
    ).astype(jnp.bfloat16)
    stacked = jnp.concatenate([token_rows, grad_rows], axis=1)
    placed = jnp.dot(chooser, stacked, preferred_element_type=jnp.float32).astype(jnp.bfloat16)
    slot_width = capacity * 2 * model_width
    plain_slots = placed.reshape(ctx_count, group_count, slot_width)
    middle = lax.all_to_all(plain_slots, "ctx", split_axis=0, concat_axis=0, tiled=True)
    shaped = middle.reshape(ctx_count, group_count, 1, slot_width)
    widened = jnp.broadcast_to(shaped, (ctx_count, group_count, SHARDS, slot_width))
    arrived = lax.all_to_all(
        widened.reshape(ctx_count, exp_count, slot_width),
        "exp",
        split_axis=1,
        concat_axis=1,
        tiled=True,
    )
    arrived = arrived.reshape(-1, 2 * model_width)
    expert_rows = arrived[:, :model_width]
    row_grads = arrived[:, model_width:]
    gate_pre = jnp.einsum("rd,fd->rf", expert_rows, w_gate, preferred_element_type=jnp.float32)
    up_pre = jnp.einsum("rd,fd->rf", expert_rows, w_up, preferred_element_type=jnp.float32)
    sigmoid_gate = jax.nn.sigmoid(gate_pre)
    activation = gate_pre * sigmoid_gate
    hidden = (activation * up_pre).astype(jnp.bfloat16)
    piece_out = jnp.einsum("rf,fd->rd", hidden, w_down, preferred_element_type=jnp.float32).astype(
        jnp.bfloat16
    )
    out_width = capacity * model_width
    piece_out = piece_out.reshape(ctx_count, exp_count, out_width)
    by_piece = lax.all_to_all(piece_out, "exp", split_axis=1, concat_axis=1, tiled=True)
    piece_sums = jnp.sum(
        by_piece.astype(jnp.float32).reshape(ctx_count, group_count, SHARDS, out_width), axis=2
    )
    expert_sums = lax.all_to_all(
        piece_sums.astype(jnp.bfloat16), "ctx", split_axis=0, concat_axis=0, tiled=True
    ).astype(piece_sums.dtype)
    expert_sums = expert_sums.reshape(expert_total * capacity, model_width)
    hidden_grad = jnp.einsum("rd,fd->rf", row_grads, w_down, preferred_element_type=jnp.float32)
    gate_cot = (
        hidden_grad * up_pre * sigmoid_gate * (1.0 + gate_pre * (1.0 - sigmoid_gate))
    ).astype(jnp.bfloat16)
    up_cot = (hidden_grad * activation).astype(jnp.bfloat16)
    grad_down = jnp.einsum(
        "rf,rd->fd", hidden, row_grads, preferred_element_type=jnp.float32
    ).astype(jnp.bfloat16)
    grad_gate = jnp.einsum(
        "rf,rd->fd", gate_cot, expert_rows, preferred_element_type=jnp.float32
    ).astype(jnp.bfloat16)
    grad_up = jnp.einsum(
        "rf,rd->fd", up_cot, expert_rows, preferred_element_type=jnp.float32
    ).astype(jnp.bfloat16)
    picked = jnp.take(expert_sums, position, axis=0)
    combined = jnp.sum((gate_flat[:, None] * picked).reshape(local_tokens, 2, model_width), axis=1)
    layer_out = (mixed + combined).astype(jnp.bfloat16)[None]
    return (layer_out, grad_gate, grad_up, grad_down)


def solution(mesh):
    placed = (
        P("exp", "ctx", None),
        P("exp", "ctx", None),
        P("exp", "ctx", None),
        P("exp", "ctx", None),
        P(),
        P("exp", None),
        P("exp", None),
        P("exp", "ctx", None),
        P("exp", "ctx", None),
        P(("ctx", "exp"), None),
        P(("ctx", "exp"), None),
        P(("ctx", "exp"), None),
        P("exp", "ctx", None),
    )
    return jax.shard_map(
        per_device,
        mesh=mesh,
        in_specs=placed,
        out_specs=(
            P("exp", "ctx", None),
            P(("ctx", "exp"), None),
            P(("ctx", "exp"), None),
            P(("ctx", "exp"), None),
        ),
        check_vma=False,
    )
```

profile of v0, /device:TPU:1, one launch (start us, length us, event | category | flops | bytes accessed | tf_op | source)
XLA Modules:
  0.0 742.1 jit_solution(3102636036667470510)
XLA Ops:
  7.2 1.9 copy.84
  9.2 0.7 all-gather.7.cloned.1.call-update
  9.9 0.8 copy.89
  10.7 0.1 eq.39
  10.9 0.1 reshape_squeeze.7
  11.0 1.0 copy.102
  12.0 0.6 reduce-window.6
  12.6 0.2 slice_reduce_fusion
  12.8 0.6 slice.13
  13.4 0.1 bitcast_convert_fusion
  13.5 2.5 broadcast_in_dim.36
  16.0 2.7 convert_element_type.81
  18.8 0.1 copy.94
  18.9 0.7 mul.118
  19.6 0.8 fusion.48
  20.4 1.8 multiply_convert_fusion
  22.2 35.1 %all-gather.5.cloned.1.call-done = bf16[1,1024,1024]{1,2,0:T(8,128)(2,1)} async-done(((bf16[1,128,1024]{1,2,0:T(8,128)(2,1)}), bf16[1,1024,1024]{1,2,0:T(8,128)(2,1)}) %all-gather.5.cloned.1.call-update) | async-done | bytes 2097168 | tf_op jit(solution)/shard_map/all_gather | solution.py:36
  57.3 2.4 multiply_reduce_fusion
  59.7 1.9 copy-done.1
  61.6 0.9 fusion.12
  62.5 40.5 %all-gather.7.cloned.1.call-done = bf16[1,1024,1024]{2,1,0:T(8,128)(2,1)} async-done(((bf16[1,128,1024]{2,1,0:T(8,128)(2,1)}), bf16[1,1024,1024]{2,1,0:T(8,128)(2,1)}) %all-gather.7.cloned.1.call-update) | async-done | bytes 2097168 | tf_op jit(solution)/shard_map/all_gather | solution.py:37
  103.1 2.9 copy.87
  106.0 3.4 fusion.37
  109.4 0.1 copy-done.5
  109.5 0.8 multiply_reduce_fusion.2
  110.4 0.2 add_convert_fusion.1
  110.6 0.6 broadcast_in_dim.35
  111.2 1.2 reshape.142
  112.4 4.2 convolution_convert_fusion.1
  116.6 6.3 reshape.143
  122.9 35.0 %all_to_all.20 = bf16[8,8,24576]{2,1,0:T(8,128)(2,1)S(1)} all-to-all(bf16[8,8,24576]{2,1,0:T(8,128)(2,1)} %reshape.143), channel_id=1, replica_groups=mesh['ctx'=8,'exp'=32] {'ctx'}, dimensions={0} | all-to-all | bytes 6291456 | tf_op jit(solution)/shard_map/all_to_all | solution.py:85
  157.9 3.4 copy.95
  161.2 8.0 %broadcast_in_dim.37 = bf16[8,8,4,24576]{3,0,2,1:T(8,128)(2,1)} broadcast(bf16[8,8,24576]{2,0,1:T(8,128)(2,1)} %copy.95), dimensions={0,1,3} | broadcast | bytes 15728640 | tf_op jit(solution)/shard_map/broadcast_in_dim | solution.py:87
  169.2 292.4 %all_to_all.21 = bf16[8,32,24576]{2,0,1:T(8,128)(2,1)S(1)} all-to-all(bf16[8,32,24576]{2,0,1:T(8,128)(2,1)} %bitcast.62), channel_id=1, replica_groups=mesh['ctx'=8,'exp'=32] {'exp'}, dimensions={1} | all-to-all | bytes 25165824 | tf_op jit(solution)/shard_map/all_to_all | solution.py:88
  461.7 19.8 %copy.96 = bf16[8,32,24576]{2,1,0:T(8,128)(2,1)} copy(bf16[8,32,24576]{2,0,1:T(8,128)(2,1)S(1)} %all_to_all.21) | data formatting | bytes 25165824 | tf_op jit(solution)/shard_map/all_to_all | solution.py:88
  481.5 20.7 %reshape.145 = bf16[1536,4096]{1,0:T(8,128)(2,1)} reshape(bf16[8,32,24576]{2,1,0:T(8,128)(2,1)} %copy.96) | data formatting | bytes 25165824 | tf_op jit(solution)/shard_map/reshape | solution.py:95
  502.3 4.9 fusion.10
  507.1 1.5 copy-done.2
  508.6 0.2 copy-done.11
  508.9 3.4 multiply_convert_fusion.3
  512.2 4.4 convolution_convert_fusion
  516.7 12.5 %reshape.146 = bf16[8,32,12288]{2,1,0:T(8,128)(2,1)} reshape(bf16[1536,2048]{1,0:T(8,128)(2,1)} %convolution_convert_fusion) | data formatting | bytes 12582912 | tf_op jit(solution)/shard_map/reshape | solution.py:107
  529.2 8.8 %copy.97 = bf16[8,32,12288]{2,0,1:T(8,128)(2,1)} copy(bf16[8,32,12288]{2,1,0:T(8,128)(2,1)} %reshape.146) | data formatting | bytes 12582912 | tf_op jit(solution)/shard_map/reshape | solution.py:107
  538.0 5.8 all-to-all-start.2
  543.9 0.1 reduce_sum.51
  544.0 0.1 copy.99
  544.2 0.1 mul.123
  544.3 0.1 copy.92
  544.4 0.1 copy.93
  544.5 0.1 copy.88
  544.7 139.6 %all-to-all-done.2 = bf16[8,32,12288]{2,0,1:T(8,128)(2,1)} async-done(((bf16[8,32,12288]{2,0,1:T(8,128)(2,1)}), bf16[8,32,12288]{2,0,1:T(8,128)(2,1)}, u32[]{:S(2)}, u32[]{:S(2)}) %all-to-all-start.2) | async-done | bytes 6291488 | tf_op jit(solution)/shard_map/all_to_all | solution.py:108
  684.3 3.7 bitcast_reduce_fusion
  688.0 2.0 copy.98
  690.0 4.3 all-to-all-start.3
  694.4 5.7 fusion.20
  700.1 4.8 fusion.2
  705.0 2.9 fusion.17
  707.9 3.2 fusion.14
  711.0 3.9 all-to-all-done.3
  714.9 4.4 reshape.154
  719.3 5.5 gather_fusion
  724.8 3.5 gather.7
  728.3 5.7 multiply_reduce_fusion.1
  734.0 0.9 fusion.41
  (46 shorter events, 0.3 us)
Async XLA Ops:
  7.2 505.1 %copy-start = (bf16[256,2048]{1,0:T(8,128)(2,1)S(1)}, bf16[256,2048]{1,0:T(8,128)(2,1)}, u32[]{:S(2)}) copy-start(bf16[256,2048]{1,0:T(8,128)(2,1)} %param.24) | copy-start | bytes 3145732
  7.2 6.2 copy-start.4
  7.2 50.1 %all-gather.5.cloned.1.call-start = ((), (), s32[]{:S(2)}) async-start(), calls=%async_computation.4 | async-start | bytes 2359296 | tf_op jit(solution)/shard_map/all_gather | solution.py:36
  9.2 93.9 %all-gather.7.cloned.1.call-start = ((), (), s32[]{:S(2)}) async-start(), calls=%async_computation.5 | async-start | bytes 2359296 | tf_op jit(solution)/shard_map/all_gather | solution.py:37
  16.0 2.7 copy-start.9
  16.0 4.3 copy-start.8
  59.7 1.9 copy-start.1
  105.9 3.5 copy-start.3
  106.0 3.6 copy-start.5
  109.5 0.8 copy-start.7
  481.5 20.7 %copy-start.10 = (bf16[256,2048]{1,0:T(8,128)(2,1)S(1)}, bf16[256,2048]{1,0:T(8,128)(2,1)}, u32[]{:S(2)}) copy-start(bf16[256,2048]{1,0:T(8,128)(2,1)} %param.22) | copy-start | bytes 3145732
  502.3 6.4 copy-start.2
  502.3 6.6 copy-start.11
  508.9 3.4 copy-start.12
  538.0 6.0 copy-start.6
  538.0 146.2 %all-to-all-start.2 = ((bf16[8,32,12288]{2,0,1:T(8,128)(2,1)}), bf16[8,32,12288]{2,0,1:T(8,128)(2,1)}, u32[]{:S(2)}, u32[]{:S(2)}) async-start(bf16[8,32,12288]{2,0,1:T(8,128)(2,1)} %copy.97), calls=%async_computation.2 | async-start | bytes 12582912 | tf_op jit(solution)/shard_map/all_to_all | solution.py:108
  690.0 24.9 %all-to-all-start.3 = ((bf16[8,8,12288]{2,1,0:T(8,128)(2,1)}), bf16[8,8,12288]{2,1,0:T(8,128)(2,1)}, u32[]{:S(2)}, u32[]{:S(2)}) async-start(bf16[8,8,12288]{2,1,0:T(8,128)(2,1)} %copy.98), calls=%async_computation.3 | async-start | bytes 3145728 | tf_op jit(solution)/shard_map/all_to_all | solution.py:112
  694.3 10.6 %slice-start = ((s8[12582912]{0:T(1024)(128)(4,1)}), s8[4194304]{0:T(1024)(128)(4,1)S(1)}, s32[]{:S(2)}) async-start(s8[12582912]{0:T(1024)(128)(4,1)} %bitcast.63), calls=%async_computation.6 | async-start | bytes 8388608
  694.3 10.6 %slice-start.1 = ((s8[12582912]{0:T(1024)(128)(4,1)}), s8[4194304]{0:T(1024)(128)(4,1)S(1)}, s32[]{:S(2)}) async-start(s8[12582912]{0:T(1024)(128)(4,1)} %bitcast.63), calls=%async_computation.7 | async-start | bytes 8388608
  700.1 4.9 slice-start.2
  700.1 4.9 copy-start.13
  705.0 2.9 copy-start.14
Sparse Core Ops, SparseCore 0:
  10.3 46.9 all-gather.4
  59.1 43.9 all-gather.6
where the time goes:
time: 751 us; the launch traced here: 742 us
  blocking collectives  327 us (44%)
  waiting for transfers between devices  220 us (29%)
  local copies, waits for them, and re-layouts  115 us (15%)
  matrix products  40 us (5%)
  other arithmetic  14.9 us (2%)
  between operations  14.8 us (2%)
  starting transfers between devices  10.2 us (1%)
    all_to_all x1, blocking collectives, per_device(): lax.all_to_all(widened.reshape(ctx_count, exp_count, slot_width), 'exp',...  292 us
    all_to_all x1, waiting for transfers between devices, per_device(): lax.all_to_all(piece_out, 'exp', split_axis=1, concat_axis=1, tiled=True)  140 us
    all_gather x1, waiting for transfers between devices, per_device(): lax.all_gather(value_rows, 'ctx', axis=0, tiled=True).reshape(-1, HEADS, HD)  40.5 us
    all_gather x1, waiting for transfers between devices, per_device(): lax.all_gather(key_rows, 'ctx', axis=0, tiled=True).reshape(-1, HEADS, HD)  35.1 us
    all_to_all x1, blocking collectives, per_device(): lax.all_to_all(plain_slots, 'ctx', split_axis=0, concat_axis=0, tiled=True)  35 us
    reshape x2, local copies, waits for them, and re-layouts, per_device(): piece_out = piece_out.reshape(ctx_count, exp_count, out_width)  21.4 us
    reshape x1, local copies, waits for them, and re-layouts, per_device(): arrived = arrived.reshape(-1, 2 * model_width)  20.7 us
    all_to_all x1, local copies, waits for them, and re-layouts, per_device(): lax.all_to_all(widened.reshape(ctx_count, exp_count, slot_width), 'exp',...  19.8 us
  transfers between devices with their start and end apart: 4, of which 4 were waited for; matrix products, arithmetic and copies ran while one was open for 4% of the time, Pallas kernels for 0%

commit v1 on v0

v1 whole, which is shorter than its diff:
```python
import jax
import jax.numpy as jnp
from jax import lax
from jax.experimental import pallas as pl
from jax.experimental.pallas import tpu as pltpu
from jax.sharding import PartitionSpec as P

HEADS = 8
HD = 128
SHARDS = 4
CAP = 6
YN = 4
MSGS = 16
ROWS = YN * CAP
MESH = pl.DeviceIdType.MESH
BF = jnp.bfloat16
F32 = jnp.float32
VMEM = pl.BlockSpec(memory_space=pltpu.VMEM)
DMA = pltpu.SemaphoreType.DMA


def coords():
    c = lax.axis_index("ctx")
    e = lax.axis_index("exp")
    z = lax.div(e, 8) * 2 + lax.div(c, 4)
    return z, lax.rem(c, 4), lax.rem(lax.div(e, 2), 4), lax.rem(e, 2)


def dev(z, y, x, core):
    return {"ctx": lax.rem(z, 2) * 4 + y, "exp": lax.div(z, 2) * 8 + x * 2 + core}


def offset(k):
    t = lax.div(k, 2)
    odd = lax.rem(t, 2)
    dz = odd * lax.div(t + 1, 2) + (1 - odd) * lax.rem(8 - lax.div(t, 2), 8)
    return dz, lax.rem(k, 2)


def dest(k):
    z, y, x, core = coords()
    dz, a = offset(k)
    return dev(lax.rem(z + dz, 8), y, x + a * (3 - 2 * x), core)


def source(k):
    z, y, x, core = coords()
    dz, a = offset(k)
    return dev(lax.rem(z + 8 - dz, 8), y, x + a * (3 - 2 * x), core)


def core_mate():
    z, y, x, core = coords()
    return dev(z, y, x, 1 - core)


def x_mate():
    z, y, x, core = coords()
    return dev(z, y, x + 1 - 2 * lax.rem(x, 2), core)


def z_mate():
    z, y, x, core = coords()
    return dev(z + 1 - 2 * lax.rem(z, 2), y, x, core)


def y_peer(step):
    z, y, x, core = coords()
    return dev(z, lax.rem(y + step, 4), x, core)


def enter():
    barrier = pltpu.get_barrier_semaphore()

    def greet(device):
        pl.semaphore_signal(barrier, inc=1, device_id=device, device_id_type=MESH)

    greet(core_mate())
    greet(x_mate())
    for step in (1, 2, 3):
        greet(y_peer(step))
    lax.fori_loop(1, MSGS, lambda k, s: (greet(dest(k)), s)[1], 0)
    pl.semaphore_wait(barrier, 5 + MSGS - 1)


def remote(src, dst, send, recv, device):
    return pltpu.make_async_remote_copy(
        src_ref=src, dst_ref=dst, send_sem=send, recv_sem=recv, device_id=device, device_id_type=MESH
    )


def each(lower, upper, body):
    def step(k, carry):
        body(k)
        return carry

    lax.fori_loop(lower, upper, step, 0)


class Dispatch:
    def __init__(self, src, out, send, recv):
        self.src, self.out = src, out
        self.send, self.recv = send, recv

    def first(self, k):
        return remote(self.src.at[k], self.out.at[0, k], self.send.at[0, k], self.recv.at[0, k], dest(k))

    def to_core(self, k):
        return remote(self.out.at[0, k], self.out.at[1, k], self.send.at[1, k], self.recv.at[1, k], core_mate())

    def to_x(self, k):
        return remote(self.out.at[0, k], self.out.at[2, k], self.send.at[2, k], self.recv.at[2, k], x_mate())

    def onward(self, k):
        return remote(self.out.at[2, k], self.out.at[3, k], self.send.at[3, k], self.recv.at[3, k], core_mate())

    def start(self):
        each(1, MSGS, lambda k: self.first(k).start())
        self.out[0, 0] = self.src[0]

    def spread(self):
        self.to_core(0).start()
        self.to_x(0).start()

        def step(k):
            self.first(k).wait_recv()
            self.to_core(k).start()
            self.to_x(k).start()
            self.to_x(k - 1).wait_recv()
            self.onward(k - 1).start()

        each(1, MSGS, step)
        self.to_x(MSGS - 1).wait_recv()
        self.onward(MSGS - 1).start()

    def finish(self):
        def step(k):
            self.to_core(k).wait_recv()
            self.onward(k).wait_recv()
            self.to_core(k).wait_send()
            self.to_x(k).wait_send()
            self.onward(k).wait_send()

        each(0, MSGS, step)
        each(1, MSGS, lambda k: self.first(k).wait_send())


class Ring:
    def __init__(self, src, own, left, right, far, send, recv):
        self.up = remote(src, left, send.at[0], recv.at[0], y_peer(1))
        self.down = remote(src, right, send.at[1], recv.at[1], y_peer(3))
        self.up2 = remote(own(1, 0), far(0), send.at[2], recv.at[2], y_peer(1))
        self.down2 = remote(own(2, 1), far(1), send.at[3], recv.at[3], y_peer(3))

    def start(self):
        self.up.start()
        self.down.start()

    def middle(self):
        self.up.wait_recv()
        self.up2.start()
        self.down.wait_recv()
        self.down2.start()

    def finish(self):
        self.up2.wait_recv()
        self.down2.wait_recv()

    def drain(self):
        for copy in (self.up, self.down, self.up2, self.down2):
            copy.wait_send()


def row_ring(src, buf, send, recv):
    half = src.shape[0] // 2
    n = src.shape[0]

    def piece(block, h):
        return buf.at[pl.ds(block * n + h * half, half)]

    return Ring(
        src,
        piece,
        buf.at[pl.ds(n, n)],
        buf.at[pl.ds(2 * n, n)],
        lambda h: piece(3, h),
        send,
        recv,
    )


def kv_ring(src, buf, base, send, recv):
    return Ring(
        src,
        lambda block, h: buf.at[base + block, h],
        buf.at[base + 1],
        buf.at[base + 2],
        lambda h: buf.at[base + 3, h],
        send,
        recv,
    )


def place(chooser, tokens, scale, placed):
    width = 512

    def step(j):
        cols = pl.ds(pl.multiple_of(j * width, width), width)
        rows = jnp.dot(chooser[...], tokens[:, cols], preferred_element_type=F32)
        if scale is not None:
            rows = rows * scale[...]
        for k in range(MSGS):
            placed[k, :, cols] = rows[k * ROWS : (k + 1) * ROWS].astype(BF)

    each(0, tokens.shape[1] // width, step)


def first_kernel(
    kv, og, pos, gts, want, kvout, cot, chooser, weight,
    ogall, posall, gall, scale, placed,
    kv_s, kv_r, og_s, og_r, small_s, small_r, d_s, d_r,
):
    enter()
    small = []
    for n, (src, buf) in enumerate(((pos, posall), (gts, gall))):
        for step in (1, 2, 3):
            sem = n * 3 + step - 1
            small.append(remote(src, buf.at[step], small_s.at[sem], small_r.at[sem], y_peer(step)))
    for copy in small:
        copy.start()
    og_ring = row_ring(og, ogall, og_s, og_r)
    og_ring.start()
    zed = remote(kv, kvout.at[4], kv_s.at[0, 4], kv_r.at[0, 4], z_mate())
    zed.start()
    near = kv_ring(kv, kvout, 0, kv_s.at[0], kv_r.at[0])
    near.start()
    n = og.shape[0]
    ogall[0:n] = og[...]
    kvout[0] = kv[...]
    posall[0] = pos[...]
    gall[0] = gts[...]
    og_ring.middle()
    for copy in small:
        copy.wait_recv()
    total = jnp.zeros((MSGS * ROWS, 1), F32)
    for block, slot in ((0, 0), (1, 1), (2, 3), (3, 2)):
        shift = block * (64 * CAP)
        hit0 = want[...] == posall[slot, 0:1, :] + shift
        hit1 = want[...] == posall[slot, 1:2, :] + shift
        gate = jnp.where(hit0, gall[slot, 0:1, :], 0.0) + jnp.where(hit1, gall[slot, 1:2, :], 0.0)
        picks = jnp.where(hit0, 1.0, 0.0) + jnp.where(hit1, 1.0, 0.0)
        chooser[:, block * n : (block + 1) * n] = picks.astype(BF)
        weight[:, block * n : (block + 1) * n] = gate
        total = total + jnp.sum(gate, axis=1, keepdims=True)
    scale[...] = total
    near.middle()
    og_ring.finish()
    place(chooser, ogall, scale, placed)
    sends = Dispatch(placed, cot, d_s, d_r)
    sends.start()
    zed.wait_recv()
    other = kv_ring(kvout.at[4], kvout, 4, kv_s.at[1], kv_r.at[1])
    other.start()
    other.middle()
    near.finish()
    other.finish()
    sends.spread()
    sends.finish()
    og_ring.drain()
    near.drain()
    other.drain()
    zed.wait_send()
    for copy in small:
        copy.wait_send()


def normed_kernel(normed, chooser, out, all_rows, placed, y_s, y_r, d_s, d_r):
    enter()
    ring = row_ring(normed, all_rows, y_s, y_r)
    ring.start()
    all_rows[0 : normed.shape[0]] = normed[...]
    ring.middle()
    ring.finish()
    place(chooser, all_rows, None, placed)
    sends = Dispatch(placed, out, d_s, d_r)
    sends.start()
    sends.spread()
    sends.finish()
    ring.drain()


def return_kernel(
    parts, hi, lo, out,
    from_core, from_diag, pair, from_x, summed, back, flat, partial, peers,
    c_s, c_r, b_s, b_r, p_s, p_r,
):
    enter()

    def mate_own(k):
        return remote(parts.at[1, k], from_core.at[k], c_s.at[0, k], c_r.at[0, k], core_mate())

    def mate_diag(k):
        return remote(parts.at[3, k], from_diag.at[k], c_s.at[1, k], c_r.at[1, k], core_mate())

    def across(k):
        return remote(pair.at[k], from_x.at[k], c_s.at[2, k], c_r.at[2, k], x_mate())

    def home(k):
        return remote(summed.at[k], back.at[k], b_s.at[k], b_r.at[k], source(k))

    def begin(k):
        mate_diag(k).start()
        mate_own(k).start()

    each(0, MSGS, begin)

    def add_pair(k):
        mate_diag(k).wait_recv()
        pair[k] = (parts[2, k].astype(F32) + from_diag[k].astype(F32)).astype(BF)
        across(k).start()

    each(0, MSGS, add_pair)

    def total(k):
        mate_own(k).wait_recv()
        across(k).wait_recv()
        rows = parts[0, k].astype(F32) + from_core[k].astype(F32) + from_x[k].astype(F32)
        return rows.astype(BF)

    flat[0:ROWS] = total(0).astype(F32)

    def send_home(k):
        summed[k] = total(k)
        home(k).start()

    each(1, MSGS, send_home)

    def take(k):
        home(k).wait_recv()
        flat[pl.ds(pl.multiple_of(k * ROWS, 8), ROWS)] = back[k].astype(F32)

    each(1, MSGS, take)

    n = out.shape[0]
    width = 512
    steps = {1: 3, 2: 1, 3: 2}

    def to_peer(block):
        return remote(
            partial.at[block - 1], peers.at[block - 1], p_s.at[block - 1], p_r.at[block - 1], y_peer(steps[block])
        )

    for block in (3, 1, 2, 0):
        mine = slice(block * n, (block + 1) * n)

        def column(j):
            cols = pl.ds(pl.multiple_of(j * width, width), width)
            rows = flat[:, cols].astype(BF)
            value = jnp.dot(hi[mine], rows, preferred_element_type=F32) + jnp.dot(
                lo[mine], rows, preferred_element_type=F32
            )
            if block:
                partial[block - 1, :, cols] = value.astype(BF)
            else:
                out[:, cols] = value

        each(0, out.shape[1] // width, column)
        if block:
            to_peer(block).start()
    for block in (1, 2, 3):
        to_peer(block).wait_recv()
        out[...] += peers[block - 1].astype(F32)
    for block in (1, 2, 3):
        to_peer(block).wait_send()

    def drain(k):
        mate_diag(k).wait_send()
        mate_own(k).wait_send()
        across(k).wait_send()

    each(0, MSGS, drain)
    each(1, MSGS, lambda k: home(k).wait_send())


def call(kernel, number, outs, scratch, args):
    return pl.pallas_call(
        kernel,
        out_shape=outs,
        in_specs=[VMEM] * len(args),
        out_specs=jax.tree.map(lambda _: VMEM, outs),
        scratch_shapes=scratch,
        compiler_params=pltpu.CompilerParams(
            collective_id=number, has_side_effects=True, vmem_limit_bytes=60 << 20
        ),
    )(*args)


def per_device(
    tokens,
    queries,
    keys,
    values,
    out_proj,
    mod_scale,
    mod_shift,
    expert_ids,
    gates,
    w_gate,
    w_up,
    w_down,
    out_grad,
):
    n = tokens.shape[1]
    width = tokens.shape[2]
    inner = queries.shape[2]
    rows = MSGS * ROWS
    z, y, x, _ = coords()
    chosen = expert_ids[0].reshape(-1)
    one_hot = (chosen[:, None] == jnp.arange(64, dtype=jnp.int32)[None, :]).astype(jnp.int32)
    before = jnp.cumsum(one_hot, axis=0) - one_hot
    position = (chosen * CAP + jnp.sum(one_hot * before, axis=1)).reshape(n, 2)
    pos = jnp.pad(position.T, ((0, 6), (0, 0)))
    gts = jnp.pad(gates[0].T, ((0, 6), (0, 0)))
    row = jnp.arange(rows, dtype=jnp.int32)
    dz, a = offset(row // ROWS)
    to_z = (z + dz) % 8
    to_x = x + a * (3 - 2 * x)
    expert = ((to_z % 2) * 4 + y) * 8 + (to_z // 2) * 2 + to_x // 2
    want = (row % ROWS // CAP) * (64 * CAP) + expert * CAP + row % CAP
    want = jnp.broadcast_to(want[:, None], (rows, n))

    kv, cot, chooser, weight = call(
        first_kernel,
        1,
        (
            jax.ShapeDtypeStruct((8, 2, n, inner), BF),
            jax.ShapeDtypeStruct((4, MSGS, ROWS, width), BF),
            jax.ShapeDtypeStruct((rows, YN * n), BF),
            jax.ShapeDtypeStruct((rows, YN * n), F32),
        ),
        [
            pltpu.VMEM((YN * n, width), BF),
            pltpu.VMEM((YN, 8, n), jnp.int32),
            pltpu.VMEM((YN, 8, n), F32),
            pltpu.VMEM((rows, 1), F32),
            pltpu.VMEM((MSGS, ROWS, width), BF),
            DMA((2, 5)),
            DMA((2, 5)),
            DMA((4,)),
            DMA((4,)),
            DMA((6,)),
            DMA((6,)),
            DMA((4, MSGS)),
            DMA((4, MSGS)),
        ],
        (jnp.stack([keys[0], values[0]]), out_grad[0], pos, gts, want),
    )
    weight = weight.T
    hi = weight.astype(BF)
    lo = (weight - hi.astype(F32)).astype(BF)

    query_heads = queries[0].reshape(n, HEADS, HD)
    key_heads = kv[:, 0].reshape(8 * n, HEADS, HD)
    value_heads = kv[:, 1].reshape(8 * n, HEADS, HD)
    scores = jnp.einsum("qhd,khd->hqk", query_heads, key_heads, preferred_element_type=F32) * HD ** (-0.5)
    exponent = jnp.exp(scores - jnp.max(scores, axis=-1)[..., None])
    accum = jnp.einsum("hqk,khd->hqd", exponent.astype(BF), value_heads, preferred_element_type=F32)
    attended = (
        jnp.transpose(accum / jnp.sum(exponent, axis=-1)[..., None], (1, 0, 2)).reshape(n, inner).astype(BF)
    )
    mixed = tokens[0].astype(F32) + jnp.dot(attended, out_proj, preferred_element_type=F32)
    mean_square = jnp.mean(mixed * mixed, axis=-1, keepdims=True)
    normed = (mixed * lax.rsqrt(mean_square + 1e-06) * (1.0 + mod_scale) + mod_shift).astype(BF)

    expert_in = call(
        normed_kernel,
        2,
        jax.ShapeDtypeStruct((4, MSGS, ROWS, width), BF),
        [
            pltpu.VMEM((YN * n, width), BF),
            pltpu.VMEM((MSGS, ROWS, width), BF),
            DMA((4,)),
            DMA((4,)),
            DMA((4, MSGS)),
            DMA((4, MSGS)),
        ],
        (normed, chooser),
    )
    expert_rows = expert_in.reshape(4 * rows, width)
    row_grads = cot.reshape(4 * rows, width)
    gate_pre = jnp.einsum("rd,fd->rf", expert_rows, w_gate, preferred_element_type=F32)
    up_pre = jnp.einsum("rd,fd->rf", expert_rows, w_up, preferred_element_type=F32)
    sigmoid_gate = jax.nn.sigmoid(gate_pre)
    activation = gate_pre * sigmoid_gate
    hidden = (activation * up_pre).astype(BF)
    piece_out = jnp.einsum("rf,fd->rd", hidden, w_down, preferred_element_type=F32).astype(BF)
    block = pltpu.VMEM((MSGS, ROWS, width), BF)
    combined = call(
        return_kernel,
        3,
        jax.ShapeDtypeStruct((n, width), F32),
        [
            block,
            block,
            block,
            block,
            block,
            block,
            pltpu.VMEM((rows, width), F32),
            pltpu.VMEM((3, n, width), BF),
            pltpu.VMEM((3, n, width), BF),
            DMA((3, MSGS)),
            DMA((3, MSGS)),
            DMA((MSGS,)),
            DMA((MSGS,)),
            DMA((3,)),
            DMA((3,)),
        ],
        (piece_out.reshape(4, MSGS, ROWS, width), hi, lo),
    )
    hidden_grad = jnp.einsum("rd,fd->rf", row_grads, w_down, preferred_element_type=F32)
    gate_cot = (hidden_grad * up_pre * sigmoid_gate * (1.0 + gate_pre * (1.0 - sigmoid_gate))).astype(BF)
    up_cot = (hidden_grad * activation).astype(BF)
    grad_down = jnp.einsum("rf,rd->fd", hidden, row_grads, preferred_element_type=F32).astype(BF)
    grad_gate = jnp.einsum("rf,rd->fd", gate_cot, expert_rows, preferred_element_type=F32).astype(BF)
    grad_up = jnp.einsum("rf,rd->fd", up_cot, expert_rows, preferred_element_type=F32).astype(BF)
    layer_out = (mixed + combined).astype(BF)[None]
    return (layer_out, grad_gate, grad_up, grad_down)


def solution(mesh):
    placed = (
        P("exp", "ctx", None),
        P("exp", "ctx", None),
        P("exp", "ctx", None),
        P("exp", "ctx", None),
        P(),
        P("exp", None),
        P("exp", None),
        P("exp", "ctx", None),
        P("exp", "ctx", None),
        P(("ctx", "exp"), None),
        P(("ctx", "exp"), None),
        P(("ctx", "exp"), None),
        P("exp", "ctx", None),
    )
    return jax.shard_map(
        per_device,
        mesh=mesh,
        in_specs=placed,
        out_specs=(
            P("exp", "ctx", None),
            P(("ctx", "exp"), None),
            P(("ctx", "exp"), None),
            P(("ctx", "exp"), None),
        ),
        check_vma=False,
    )
```

time: 751 us -> 322 us (0.43); the launches traced: 742 us -> 321 us
  blocking collectives: 327 us -> 0 us
  Pallas kernels: 0 us -> 276 us
  waiting for transfers between devices: 220 us -> 0 us
  local copies, waits for them, and re-layouts: 115 us -> 11 us
  matrix products: 40 us -> 24.9 us
  between operations: 14.8 us -> 0.89 us
  starting transfers between devices: 10.2 us -> 0 us
    all_to_all x2 -> x0, blocking collectives: 327 us -> none  [the longest x1 292 us: per_device(): lax.all_to_all(widened.reshape(ctx_count, exp_count, slot_width), 'exp',...]
    pallas_call x0 -> x3, Pallas kernels: none -> 276 us  [call(): pl.pallas_call(kernel, out_shape=outs, in_specs=[VMEM] * len(args), out_s...]
    all_to_all x2 -> x0, waiting for transfers between devices: 143 us -> none  [the longest x1 140 us: per_device(): lax.all_to_all(piece_out, 'exp', split_axis=1, concat_axis=1, tiled=True)]
    all_gather x2 -> x0, waiting for transfers between devices: 75.6 us -> none  [the longest x1 40.5 us: per_device(): lax.all_gather(value_rows, 'ctx', axis=0, tiled=True).reshape(-1, HEADS, HD)]
    reshape x6 -> x0, local copies, waits for them, and re-layouts: 53.9 us -> none  [the longest x2 21.4 us: per_device(): piece_out = piece_out.reshape(ctx_count, exp_count, out_width)]
    all_to_all x2 -> x0, local copies, waits for them, and re-layouts: 23.2 us -> none  [the longest x1 19.8 us: per_device(): lax.all_to_all(widened.reshape(ctx_count, exp_count, slot_width), 'exp',...]
    dot_general x11 -> x10, matrix products: 40 us -> 24.9 us  [the longest x1 4.77 us: per_device(): jnp.einsum('rd,fd->rf', expert_rows, w_gate, preferred_element_type=F32)]
    broadcast_in_dim x3 -> x1, local copies, waits for them, and re-layouts: 11.2 us -> 0.8 us  [per_device(): want = jnp.broadcast_to(want[:, None], (rows, n))]
  transfers between devices with their start and end apart: 4 -> 0, of which waited for: 4 -> 0; matrix products, arithmetic and copies ran while one was open for 4% -> 0% of each run, Pallas kernels for 0% -> 0%
where the time goes in v1:
time: 322 us; the launch traced here: 321 us
  Pallas kernels  276 us (86%)
  matrix products  24.9 us (8%)
  local copies, waits for them, and re-layouts  11 us (3%)
  other arithmetic  8.18 us (3%)
    pallas_call x3, Pallas kernels, call(): pl.pallas_call(kernel, out_shape=outs, in_specs=[VMEM] * len(args), out_s...  276 us

profile of v1, /device:TPU:1, one launch (start us, length us, event | category | flops | bytes accessed | tf_op | source)
XLA Modules:
  0.0 321.0 jit_solution(3424642272219178193)
XLA Ops:
  0.6 0.0 copy-start
  0.7 0.1 fusion.50
  0.7 0.8 broadcast_in_dim.4.want
  1.5 0.8 copy.22
  2.3 0.1 eq.34
  2.5 0.6 reduce-window.6
  3.1 0.2 slice_reduce_fusion
  3.3 0.1 eq.30
  3.4 0.1 fusion.33
  3.5 0.1 reduce_sum.30
  3.7 0.1 copy.25
  3.8 0.7 fusion.67
  4.5 0.6 pad.8.pos
  5.1 1.9 pad_maximum_fusion.kv
  6.9 1.3 pad.9.gts
  8.2 110.0 %shard_map.156 = (bf16[8,2,128,1024]{3,2,1,0:T(8,128)(2,1)}, bf16[4,16,24,2048]{3,2,1,0:T(8,128)(2,1)}, bf16[384,512]{1,0:T(8,128)(2,1)}, f32[384,512]{1,0:T(8,128)}) custom-call(bf16[2,128,1024]{2,1,0:T(8,128)(2,1)} %pad_maximum_fusion.kv, bf16[128,2048]{1,0:T(8,128)(2,1)} %bitcast.108, s32[8,128]{1,0:T(8,128)} %pad.8.pos, f32[8,128]{1,0:T(8,128)} %pad.9.gts, ...), custom_call_target="tpu_custom_call" | custom-call | tf_op jit(solution)/shard_map/pallas_call | solution.py:386
  118.2 2.7 fusion.71
  120.9 0.0 copy-start.4
  120.9 0.6 copy.34
  121.6 0.3 copy-done.4
  121.9 0.7 bitcast_reduce_fusion
  122.7 0.7 fusion.1
  123.4 0.6 copy.33
  124.0 0.0 copy-start.2
  124.0 0.0 copy-start.3
  124.0 1.3 fusion.21
  125.4 0.8 copy-done.2
  126.2 0.1 copy-done.3
  126.3 0.0 copy-start.6
  126.3 0.0 copy-start.5
  126.3 0.8 multiply_reduce_fusion
  127.1 0.0 copy-done.6
  127.2 0.0 copy-done.5
  127.2 1.0 add_convert_fusion.1.normed
  128.2 0.0 copy-start.7
  128.2 74.9 %shard_map.157 = bf16[4,16,24,2048]{3,2,1,0:T(8,128)(2,1)} custom-call(bf16[128,2048]{1,0:T(8,128)(2,1)} %add_convert_fusion.1.normed, bf16[384,512]{1,0:T(8,128)(2,1)} %get-tuple-element.9.chooser), custom_call_target="tpu_custom_call" | custom-call | tf_op jit(solution)/shard_map/pallas_call | solution.py:386
  203.1 0.0 copy-done.7
  203.1 0.0 copy-start.1
  203.1 0.0 copy-start.8
  203.1 0.0 slice-start
  203.1 4.8 %fusion.72 = f32[1536,256]{1,0:T(8,128)S(1)} fusion(bf16[1536,2048]{1,0:T(8,128)(2,1)} %bitcast.102, bf16[256,2048]{1,0:T(8,128)(2,1)S(1)} %copy-done.7), kind=kOutput, calls=%fused_computation.117 | convolution fusion | flops 1610612736 | bytes 8912896 | tf_op jit(solution)/shard_map/rd,fd->rf/dot_general | solution.py:491
  207.9 0.0 copy-done.1
  207.9 0.0 copy-done.8
  207.9 0.0 slice-start.1
  207.9 2.0 multiply_convert_fusion.2
  210.0 0.0 slice-done
  210.0 0.1 slice-done.1
  210.1 2.8 convolution_convert_fusion.1
  212.9 0.0 copy-done
  212.9 1.8 fusion.73
  214.7 2.8 convolution_convert_fusion.2
  217.6 3.0 convolution_convert_fusion.3
  220.6 4.7 %convolution_convert_fusion = bf16[1536,2048]{1,0:T(8,128)(2,1)} fusion(bf16[1536,256]{1,0:T(8,128)(2,1)S(1)} %get-tuple-element.20, bf16[256,2048]{1,0:T(8,128)(2,1)S(1)} %copy-done), kind=kOutput, calls=%fused_computation | convolution fusion | flops 1613758464 | bytes 8126464 | tf_op jit(solution)/shard_map/rf,fd->rd/dot_general | solution.py:496
  225.3 1.4 copy.30
  226.7 1.0 fusion.26
  227.7 91.2 %shard_map.158 = f32[128,2048]{1,0:T(8,128)} custom-call(bf16[4,16,24,2048]{3,2,1,0:T(8,128)(2,1)} %bitcast.94, bf16[512,384]{1,0:T(8,128)(2,1)} %get-tuple-element.13.hi, bf16[512,384]{1,0:T(8,128)(2,1)} %get-tuple-element.12.lo), custom_call_target="tpu_custom_call" | custom-call | tf_op jit(solution)/shard_map/pallas_call | solution.py:386
  318.9 2.1 fusion.28
  (7 shorter events, 0.1 us)
Async XLA Ops:
  0.6 212.3 %copy-start = (bf16[256,2048]{1,0:T(8,128)(2,1)S(1)}, bf16[256,2048]{1,0:T(8,128)(2,1)}, u32[]{:S(2)}) copy-start(bf16[256,2048]{1,0:T(8,128)(2,1)} %param.24) | copy-start | bytes 3145732
  120.9 1.0 copy-start.4
  124.0 2.2 copy-start.2
  124.0 2.3 copy-start.3
  126.3 0.8 copy-start.6
  126.3 0.9 copy-start.5
  128.2 74.9 %copy-start.7 = (bf16[256,2048]{1,0:T(8,128)(2,1)S(1)}, bf16[256,2048]{1,0:T(8,128)(2,1)}, u32[]{:S(2)}) copy-start(bf16[256,2048]{1,0:T(8,128)(2,1)} %param.22) | copy-start | bytes 3145732
  203.1 4.8 %copy-start.1 = (bf16[4,16,24,2048]{3,2,1,0:T(8,128)(2,1)S(1)}, bf16[4,16,24,2048]{3,2,1,0:T(8,128)(2,1)}, u32[]{:S(2)}) copy-start(bf16[4,16,24,2048]{3,2,1,0:T(8,128)(2,1)} %shard_map.157) | copy-start | bytes 18874372
  203.1 4.8 %copy-start.8 = (bf16[256,2048]{1,0:T(8,128)(2,1)S(1)}, bf16[256,2048]{1,0:T(8,128)(2,1)}, u32[]{:S(2)}) copy-start(bf16[256,2048]{1,0:T(8,128)(2,1)} %param.23) | copy-start | bytes 3145732
  203.1 6.9 %slice-start = ((s8[6291456]{0:T(1024)(128)(4,1)}), s8[4194304]{0:T(1024)(128)(4,1)S(1)}, s32[]{:S(2)}) async-start(s8[6291456]{0:T(1024)(128)(4,1)} %bitcast.95), calls=%async_computation | async-start | bytes 8388608
  207.9 2.2 slice-start.1

commit v2 on v1

v2 whole, which is shorter than its diff:
```python
import jax
import jax.numpy as jnp
from jax import lax
from jax.experimental import pallas as pl
from jax.experimental.pallas import tpu as pltpu
from jax.sharding import PartitionSpec as P

HEADS = 8
HD = 128
SHARDS = 4
CAP = 6
YN = 4
MSGS = 16
ROWS = YN * CAP
MESH = pl.DeviceIdType.MESH
BF = jnp.bfloat16
F32 = jnp.float32
VMEM = pl.BlockSpec(memory_space=pltpu.VMEM)
ANY = pl.BlockSpec(memory_space=pl.ANY)
DMA = pltpu.SemaphoreType.DMA


def coords():
    c = lax.axis_index("ctx")
    e = lax.axis_index("exp")
    z = lax.div(e, 8) * 2 + lax.div(c, 4)
    return z, lax.rem(c, 4), lax.rem(lax.div(e, 2), 4), lax.rem(e, 2)


def dev(z, y, x, core):
    return {"ctx": lax.rem(z, 2) * 4 + y, "exp": lax.div(z, 2) * 8 + x * 2 + core}


def offset(k):
    t = lax.div(k, 2)
    odd = lax.rem(t, 2)
    dz = odd * lax.div(t + 1, 2) + (1 - odd) * lax.rem(8 - lax.div(t, 2), 8)
    return dz, lax.rem(k, 2)


def dest(k):
    z, y, x, core = coords()
    dz, a = offset(k)
    return dev(lax.rem(z + dz, 8), y, x + a * (3 - 2 * x), core)


def source(k):
    z, y, x, core = coords()
    dz, a = offset(k)
    return dev(lax.rem(z + 8 - dz, 8), y, x + a * (3 - 2 * x), core)


def core_mate():
    z, y, x, core = coords()
    return dev(z, y, x, 1 - core)


def x_mate():
    z, y, x, core = coords()
    return dev(z, y, x + 1 - 2 * lax.rem(x, 2), core)


def z_mate():
    z, y, x, core = coords()
    return dev(z + 1 - 2 * lax.rem(z, 2), y, x, core)


def y_peer(step):
    z, y, x, core = coords()
    return dev(z, lax.rem(y + step, 4), x, core)


def enter():
    barrier = pltpu.get_barrier_semaphore()

    def greet(device):
        pl.semaphore_signal(barrier, inc=1, device_id=device, device_id_type=MESH)

    greet(core_mate())
    greet(x_mate())
    for step in (1, 2, 3):
        greet(y_peer(step))
    lax.fori_loop(1, MSGS, lambda k, s: (greet(dest(k)), s)[1], 0)
    pl.semaphore_wait(barrier, 5 + MSGS - 1)


def remote(src, dst, send, recv, device):
    return pltpu.make_async_remote_copy(
        src_ref=src, dst_ref=dst, send_sem=send, recv_sem=recv, device_id=device, device_id_type=MESH
    )


def each(lower, upper, body):
    def step(k, carry):
        body(k)
        return carry

    lax.fori_loop(lower, upper, step, 0)


class Dispatch:
    def __init__(self, src, out, cols, send, recv, local):
        self.src, self.out, self.cols = src, out, cols
        self.send, self.recv = send, recv
        self.local = pltpu.make_async_copy(src.at[0, :, cols], out.at[0, 0, :, cols], local)

    def hop(self, stage, src, block, k, device):
        return remote(
            src, self.out.at[block, k, :, self.cols], self.send.at[stage, k], self.recv.at[stage, k], device
        )

    def first(self, k):
        return self.hop(0, self.src.at[k, :, self.cols], 0, k, dest(k))

    def to_core(self, k):
        return self.hop(1, self.out.at[0, k, :, self.cols], 1, k, core_mate())

    def to_x(self, k):
        return self.hop(2, self.out.at[0, k, :, self.cols], 2, k, x_mate())

    def onward(self, k):
        return self.hop(3, self.out.at[2, k, :, self.cols], 3, k, core_mate())

    def start(self):
        self.local.start()
        each(1, MSGS, lambda k: self.first(k).start())

    def spread_own(self):
        self.local.wait()
        self.to_core(0).start()
        self.to_x(0).start()

    def spread(self, lower, upper):
        def step(k):
            self.first(k).wait_recv()
            self.to_core(k).start()
            self.to_x(k).start()
            self.to_x(k - 1).wait_recv()
            self.onward(k - 1).start()

        each(lower, upper, step)

    def spread_last(self):
        self.to_x(MSGS - 1).wait_recv()
        self.onward(MSGS - 1).start()

    def finish(self):
        def step(k):
            self.to_core(k).wait_recv()
            self.onward(k).wait_recv()
            self.to_core(k).wait_send()
            self.to_x(k).wait_send()
            self.onward(k).wait_send()

        each(0, MSGS, step)
        each(1, MSGS, lambda k: self.first(k).wait_send())


class Ring:
    def __init__(self, src, own, left, right, far, send, recv):
        self.up = remote(src, left, send.at[0], recv.at[0], y_peer(1))
        self.down = remote(src, right, send.at[1], recv.at[1], y_peer(3))
        self.up2 = remote(own(1, 0), far(0), send.at[2], recv.at[2], y_peer(1))
        self.down2 = remote(own(2, 1), far(1), send.at[3], recv.at[3], y_peer(3))

    def start(self):
        self.up.start()
        self.down.start()

    def middle(self):
        self.up.wait_recv()
        self.up2.start()
        self.down.wait_recv()
        self.down2.start()

    def finish(self):
        self.up2.wait_recv()
        self.down2.wait_recv()

    def drain(self):
        for copy in (self.up, self.down, self.up2, self.down2):
            copy.wait_send()


def row_ring(src, buf, cols, send, recv):
    n = src.shape[0]
    half = n // 2

    def piece(block, h):
        return buf.at[pl.ds(block * n + h * half, half), cols]

    return Ring(
        src.at[:, cols],
        piece,
        buf.at[pl.ds(n, n), cols],
        buf.at[pl.ds(2 * n, n), cols],
        lambda h: piece(3, h),
        send,
        recv,
    )


def kv_ring(buf, base, send, recv):
    return Ring(
        buf.at[base],
        lambda block, h: buf.at[base + block, h],
        buf.at[base + 1],
        buf.at[base + 2],
        lambda h: buf.at[base + 3, h],
        send,
        recv,
    )


def place(chooser, tokens, scale, placed, base, size):
    width = 512

    def step(j):
        cols = pl.ds(pl.multiple_of(base + j * width, width), width)
        rows = jnp.dot(chooser[...], tokens[:, cols], preferred_element_type=F32)
        if scale is not None:
            rows = rows * scale[...]
        for k in range(MSGS):
            placed[k, :, cols] = rows[k * ROWS : (k + 1) * ROWS].astype(BF)

    each(0, size // width, step)


def attend(queries, kvall, attended, h):
    cols = pl.ds(pl.multiple_of(h * HD, HD), HD)
    keys = kvall[:, 0, :, cols].reshape(-1, HD)
    values = kvall[:, 1, :, cols].reshape(-1, HD)
    scores = lax.dot_general(
        queries[:, cols], keys, (((1,), (1,)), ((), ())), preferred_element_type=F32
    ) * HD ** (-0.5)
    exponent = jnp.exp(scores - jnp.max(scores, axis=1, keepdims=True))
    total = jnp.sum(exponent, axis=1, keepdims=True)
    mixed = jnp.dot(exponent.astype(BF), values, preferred_element_type=F32)
    attended[:, cols] = (mixed / total).astype(BF)


CHUNKS = 1


def forward_kernel(
    keys, values, out_proj, og, queries, tokens, mod, small, want,
    cot, expert_in, mixed, hi, lo,
    kvall, ogall, nall, smallall, ready, scale, placed_cot, placed_in, chooser, attended, normed, proj,
    load, local, kv_s, kv_r, og_s, og_r, small_s, small_r, n_s, n_r, c_s, c_r, d_s, d_r,
):
    n, width = og.shape
    every = pl.ds(0, width)
    key_load = pltpu.make_async_copy(keys, kvall.at[0, 0], load.at[0])
    value_load = pltpu.make_async_copy(values, kvall.at[0, 1], load.at[1])
    proj_load = pltpu.make_async_copy(out_proj, proj, load.at[2])
    key_load.start()
    value_load.start()
    proj_load.start()
    names = lax.broadcasted_iota(jnp.int32, (64, n), 0).astype(F32)
    hit0 = names == small[0:1, :]
    hit1 = names == small[1:2, :]
    earlier = lax.broadcasted_iota(jnp.int32, (n, n), 0) < lax.broadcasted_iota(jnp.int32, (n, n), 1)
    named = jnp.where(hit0, 1.0, 0.0) + jnp.where(hit1, 1.0, 0.0)
    before = jnp.dot(named.astype(BF), jnp.where(earlier, 1.0, 0.0).astype(BF), preferred_element_type=F32)
    slot0 = jnp.sum(jnp.where(hit0, before, 0.0), axis=0, keepdims=True)
    slot1 = jnp.sum(jnp.where(hit1, before, 0.0), axis=0, keepdims=True)
    ready[0:1, :] = small[0:1, :] * CAP + slot0
    ready[1:2, :] = small[1:2, :] * CAP + slot1
    ready[2:8, :] = small[2:8, :]
    enter()
    og_ring = row_ring(og, ogall, every, og_s, og_r)
    og_ring.start()
    key_load.wait()
    value_load.wait()
    zed = remote(kvall.at[0], kvall.at[4], kv_s.at[0, 4], kv_r.at[0, 4], z_mate())
    zed.start()
    near = kv_ring(kvall, 0, kv_s.at[0], kv_r.at[0])
    near.start()
    small_sends = [
        remote(ready, smallall.at[step], small_s.at[step - 1], small_r.at[step - 1], y_peer(step))
        for step in (1, 2, 3)
    ]
    for copy in small_sends:
        copy.start()
    ogall[0:n] = og[...]
    smallall[0] = ready[...]
    og_ring.middle()
    zed.wait_recv()
    other = kv_ring(kvall, 4, kv_s.at[1], kv_r.at[1])
    other.start()
    for copy in small_sends:
        copy.wait_recv()
    total = jnp.zeros((MSGS * ROWS, 1), F32)
    for block, slot in ((0, 0), (1, 1), (2, 3), (3, 2)):
        shift = float(block * 64 * CAP)
        hit0 = want[...] == smallall[slot, 0:1, :] + shift
        hit1 = want[...] == smallall[slot, 1:2, :] + shift
        gate = jnp.where(hit0, smallall[slot, 2:3, :], 0.0) + jnp.where(hit1, smallall[slot, 3:4, :], 0.0)
        picks = jnp.where(hit0, 1.0, 0.0) + jnp.where(hit1, 1.0, 0.0)
        chooser[:, block * n : (block + 1) * n] = picks.astype(BF)
        turned = gate.T
        top = turned.astype(BF)
        hi[block * n : (block + 1) * n, :] = top
        lo[block * n : (block + 1) * n, :] = (turned - top.astype(F32)).astype(BF)
        total = total + jnp.sum(gate, axis=1, keepdims=True)
    scale[...] = total
    near.middle()
    og_ring.finish()
    place(chooser, ogall, scale, placed_cot, 0, width)
    cot_sends = Dispatch(placed_cot, cot, every, c_s, c_r, local.at[0])
    cot_sends.start()
    other.middle()
    cot_sends.spread_own()
    cot_sends.spread(1, 5)
    near.finish()
    other.finish()
    each(0, HEADS // 2, lambda h: attend(queries, kvall, attended, h))
    cot_sends.spread(5, 10)
    each(HEADS // 2, HEADS, lambda h: attend(queries, kvall, attended, h))
    cot_sends.spread(10, 14)
    proj_load.wait()
    part = 512
    squares = jnp.zeros((n, 1), F32)
    for j in range(width // part):
        cols = slice(j * part, (j + 1) * part)
        value = tokens[:, cols].astype(F32) + jnp.dot(
            attended[...], proj[:, cols], preferred_element_type=F32
        )
        mixed[:, cols] = value
        squares = squares + jnp.sum(value * value, axis=1, keepdims=True)
    inverse = lax.rsqrt(squares * (1.0 / width) + 1e-06)
    size = width // CHUNKS
    rings, sends = [], []
    for chunk in range(CHUNKS):
        cols = pl.ds(chunk * size, size)
        window = slice(chunk * size, (chunk + 1) * size)
        normed[:, window] = (
            mixed[:, window] * inverse * (1.0 + mod[0:1, window]) + mod[1:2, window]
        ).astype(BF)
        ring = row_ring(normed, nall, cols, n_s.at[chunk], n_r.at[chunk])
        ring.start()
        rings.append(ring)
        sends.append(Dispatch(placed_in, expert_in, cols, d_s.at[chunk], d_r.at[chunk], local.at[1 + chunk]))
    nall[0:n] = normed[...]
    cot_sends.spread(14, 16)
    cot_sends.spread_last()
    for ring in rings:
        ring.middle()
    for chunk in range(CHUNKS):
        rings[chunk].finish()
        place(chooser, nall, None, placed_in, chunk * size, size)
        sends[chunk].start()
    for chunk in range(CHUNKS):
        sends[chunk].spread_own()
        sends[chunk].spread(1, MSGS)
        sends[chunk].spread_last()
    cot_sends.finish()
    for chunk in range(CHUNKS):
        sends[chunk].finish()
        rings[chunk].drain()
    og_ring.drain()
    near.drain()
    other.drain()
    zed.wait_send()
    for copy in small_sends:
        copy.wait_send()


PARTS = 2


def expert_kernel(
    rows_in, cots_in, w_gate, w_up, w_down, hi, lo,
    out, grad_gate, grad_up, grad_down,
    rows, cots, gate, up, hidden_t, gate_t, up_t,
    pieces, from_core, from_diag, pair, from_x, summed, back, flat, partial, peers,
    load, c_s, c_r, b_s, b_r, p_s, p_r,
):
    block_rows = MSGS * ROWS
    n, width = out.shape
    size = width // PARTS
    part = 512
    order = (3, 1, 2, 0)

    def window(block):
        return pl.ds(block * block_rows, block_rows)

    row_loads = [
        pltpu.make_async_copy(rows_in.at[window(block)], rows.at[window(block)], load.at[block])
        for block in order
    ]
    cot_load = pltpu.make_async_copy(cots_in, cots, load.at[4])
    for copy in row_loads:
        copy.start()
    cot_load.start()
    enter()

    def mate_own(c, k):
        return remote(pieces.at[c, 1, k], from_core.at[c, k], c_s.at[c, 0, k], c_r.at[c, 0, k], core_mate())

    def mate_diag(c, k):
        return remote(pieces.at[c, 3, k], from_diag.at[c, k], c_s.at[c, 1, k], c_r.at[c, 1, k], core_mate())

    def across(c, k):
        return remote(pair.at[c, k], from_x.at[c, k], c_s.at[c, 2, k], c_r.at[c, 2, k], x_mate())

    def home(c, k):
        return remote(summed.at[c, k], back.at[c, k], b_s.at[c, k], b_r.at[c, k], source(k))

    across_dims = (((1,), (1,)), ((), ()))
    for block, copy in zip(order, row_loads):
        copy.wait()
        mine = window(block)
        g = lax.dot_general(rows[mine, :], w_gate[...], across_dims, preferred_element_type=F32)
        u = lax.dot_general(rows[mine, :], w_up[...], across_dims, preferred_element_type=F32)
        gate[mine, :] = g
        up[mine, :] = u
        h = g * jax.nn.sigmoid(g) * u
        hidden = h.astype(BF)
        hidden_t[:, block * block_rows : (block + 1) * block_rows] = h.T.astype(BF)
        for j in range(width // part):
            value = jnp.dot(hidden, w_down[:, j * part : (j + 1) * part], preferred_element_type=F32)
            c, base = j * part // size, j * part % size
            for k in range(MSGS):
                pieces[c, block, k, :, base : base + part] = value[k * ROWS : (k + 1) * ROWS].astype(BF)
        if block == 3:
            for c in range(PARTS):
                each(0, MSGS, lambda k: mate_diag(c, k).start())
        if block == 1:
            for c in range(PARTS):
                each(0, MSGS, lambda k: mate_own(c, k).start())

    for c in range(PARTS):

        def add_pair(k):
            mate_diag(c, k).wait_recv()
            pair[c, k] = (pieces[c, 2, k].astype(F32) + from_diag[c, k].astype(F32)).astype(BF)
            across(c, k).start()

        each(0, MSGS, add_pair)

    cot_load.wait()
    for block in range(4):
        mine = window(block)
        hidden_grad = lax.dot_general(cots[mine, :], w_down[...], across_dims, preferred_element_type=F32)
        g = gate[mine, :]
        sg = jax.nn.sigmoid(g)
        columns = slice(block * block_rows, (block + 1) * block_rows)
        gate_t[:, columns] = (hidden_grad * up[mine, :] * sg * (1.0 + g * (1.0 - sg))).T.astype(BF)
        up_t[:, columns] = (hidden_grad * (g * sg)).T.astype(BF)

    for c in range(PARTS):
        cols = slice(c * size, (c + 1) * size)

        def total(k):
            mate_own(c, k).wait_recv()
            across(c, k).wait_recv()
            value = pieces[c, 0, k].astype(F32) + from_core[c, k].astype(F32) + from_x[c, k].astype(F32)
            return value.astype(BF)

        flat[0:ROWS, cols] = total(0).astype(F32)

        def send_home(k):
            summed[c, k] = total(k)
            home(c, k).start()

        each(1, MSGS, send_home)

    def gradients(j):
        cols = pl.ds(pl.multiple_of(j * part, part), part)
        grad_down[:, cols] = jnp.dot(hidden_t[...], cots[:, cols], preferred_element_type=F32).astype(BF)
        grad_gate[:, cols] = jnp.dot(gate_t[...], rows[:, cols], preferred_element_type=F32).astype(BF)
        grad_up[:, cols] = jnp.dot(up_t[...], rows[:, cols], preferred_element_type=F32).astype(BF)

    each(0, width // part, gradients)

    steps = {1: 3, 2: 1, 3: 2}

    def to_peer(c, block):
        b = block - 1
        return remote(partial.at[c, b], peers.at[c, b], p_s.at[c, b], p_r.at[c, b], y_peer(steps[block]))

    for c in range(PARTS):
        cols = slice(c * size, (c + 1) * size)

        def take(k):
            home(c, k).wait_recv()
            flat[pl.ds(pl.multiple_of(k * ROWS, 8), ROWS), cols] = back[c, k].astype(F32)

        each(1, MSGS, take)
        for block in (3, 1, 2, 0):
            mine = slice(block * n, (block + 1) * n)
            for j in range(size // part):
                at = c * size + j * part
                values = flat[:, at : at + part].astype(BF)
                value = jnp.dot(hi[mine], values, preferred_element_type=F32) + jnp.dot(
                    lo[mine], values, preferred_element_type=F32
                )
                if block:
                    partial[c, block - 1, :, j * part : (j + 1) * part] = value.astype(BF)
                else:
                    out[:, at : at + part] = value
            if block:
                to_peer(c, block).start()
    for c in range(PARTS):
        cols = slice(c * size, (c + 1) * size)
        for block in (1, 2, 3):
            to_peer(c, block).wait_recv()
            out[:, cols] += peers[c, block - 1].astype(F32)
    for c in range(PARTS):
        for block in (1, 2, 3):
            to_peer(c, block).wait_send()

        def drain(k):
            mate_diag(c, k).wait_send()
            mate_own(c, k).wait_send()
            across(c, k).wait_send()

        each(0, MSGS, drain)
        each(1, MSGS, lambda k: home(c, k).wait_send())


def call(kernel, number, outs, scratch, args, in_specs=None, out_specs=None):
    return pl.pallas_call(
        kernel,
        out_shape=outs,
        in_specs=in_specs or [VMEM] * len(args),
        out_specs=out_specs or jax.tree.map(lambda _: VMEM, outs),
        scratch_shapes=scratch,
        compiler_params=pltpu.CompilerParams(
            collective_id=number, has_side_effects=True, vmem_limit_bytes=67043328
        ),
    )(*args)


def per_device(
    tokens,
    queries,
    keys,
    values,
    out_proj,
    mod_scale,
    mod_shift,
    expert_ids,
    gates,
    w_gate,
    w_up,
    w_down,
    out_grad,
):
    n = tokens.shape[1]
    width = tokens.shape[2]
    inner = queries.shape[2]
    rows = MSGS * ROWS
    z, y, x, _ = coords()
    small = jnp.concatenate(
        [expert_ids[0].T.astype(F32), gates[0].T, jnp.zeros((4, n), F32)], axis=0
    )
    row = jnp.arange(rows, dtype=jnp.int32)
    dz, a = offset(row // ROWS)
    to_z = (z + dz) % 8
    to_x = x + a * (3 - 2 * x)
    expert = ((to_z % 2) * 4 + y) * 8 + (to_z // 2) * 2 + to_x // 2
    want = (row % ROWS // CAP) * (64 * CAP) + expert * CAP + row % CAP
    want = jnp.broadcast_to(want.astype(F32)[:, None], (rows, n))
    mod = jnp.concatenate([mod_scale, mod_shift], axis=0)

    slots = jax.ShapeDtypeStruct((4, MSGS, ROWS, width), BF)
    routed = jax.ShapeDtypeStruct((YN * n, rows), BF)
    cot, expert_in, mixed, hi, lo = call(
        forward_kernel,
        1,
        (slots, slots, jax.ShapeDtypeStruct((n, width), F32), routed, routed),
        [
            pltpu.VMEM((8, 2, n, inner), BF),
            pltpu.VMEM((YN * n, width), BF),
            pltpu.VMEM((YN * n, width), BF),
            pltpu.VMEM((YN, 8, n), F32),
            pltpu.VMEM((8, n), F32),
            pltpu.VMEM((rows, 1), F32),
            pltpu.VMEM((MSGS, ROWS, width), BF),
            pltpu.VMEM((MSGS, ROWS, width), BF),
            pltpu.VMEM((rows, YN * n), BF),
            pltpu.VMEM((n, inner), BF),
            pltpu.VMEM((n, width), BF),
            pltpu.VMEM((inner, width), BF),
            DMA((3,)),
            DMA((1 + CHUNKS,)),
            DMA((2, 5)),
            DMA((2, 5)),
            DMA((4,)),
            DMA((4,)),
            DMA((3,)),
            DMA((3,)),
            DMA((CHUNKS, 4)),
            DMA((CHUNKS, 4)),
            DMA((4, MSGS)),
            DMA((4, MSGS)),
            DMA((CHUNKS, 4, MSGS)),
            DMA((CHUNKS, 4, MSGS)),
        ],
        (keys[0], values[0], out_proj, out_grad[0], queries[0], tokens[0], mod, small, want),
        in_specs=[ANY] * 3 + [VMEM] * 6,
        out_specs=(ANY, ANY, VMEM, VMEM, VMEM),
    )
    everything = 4 * rows
    hid = w_gate.shape[0]
    block = pltpu.VMEM((PARTS, MSGS, ROWS, width // PARTS), BF)
    share = pltpu.VMEM((PARTS, 3, n, width // PARTS), BF)
    grad = jax.ShapeDtypeStruct((hid, width), BF)
    combined, grad_gate, grad_up, grad_down = call(
        expert_kernel,
        2,
        (jax.ShapeDtypeStruct((n, width), F32), grad, grad, grad),
        [
            pltpu.VMEM((everything, width), BF),
            pltpu.VMEM((everything, width), BF),
            pltpu.VMEM((everything, hid), F32),
            pltpu.VMEM((everything, hid), F32),
            pltpu.VMEM((hid, everything), BF),
            pltpu.VMEM((hid, everything), BF),
            pltpu.VMEM((hid, everything), BF),
            pltpu.VMEM((PARTS, 4, MSGS, ROWS, width // PARTS), BF),
            block,
            block,
            block,
            block,
            block,
            block,
            pltpu.VMEM((rows, width), F32),
            share,
            share,
            DMA((5,)),
            DMA((PARTS, 3, MSGS)),
            DMA((PARTS, 3, MSGS)),
            DMA((PARTS, MSGS)),
            DMA((PARTS, MSGS)),
            DMA((PARTS, 3)),
            DMA((PARTS, 3)),
        ],
        (expert_in.reshape(everything, width), cot.reshape(everything, width), w_gate, w_up, w_down, hi, lo),
        in_specs=[ANY] * 2 + [VMEM] * 5,
    )
    layer_out = (mixed + combined).astype(BF)[None]
    return (layer_out, grad_gate, grad_up, grad_down)


def solution(mesh):
    placed = (
        P("exp", "ctx", None),
        P("exp", "ctx", None),
        P("exp", "ctx", None),
        P("exp", "ctx", None),
        P(),
        P("exp", None),
        P("exp", None),
        P("exp", "ctx", None),
        P("exp", "ctx", None),
        P(("ctx", "exp"), None),
        P(("ctx", "exp"), None),
        P(("ctx", "exp"), None),
        P("exp", "ctx", None),
    )
    return jax.shard_map(
        per_device,
        mesh=mesh,
        in_specs=placed,
        out_specs=(
            P("exp", "ctx", None),
            P(("ctx", "exp"), None),
            P(("ctx", "exp"), None),
            P(("ctx", "exp"), None),
        ),
        check_vma=False,
    )
```

time: 322 us -> 255 us (0.79)
  Pallas kernels: 276 us -> 242 us
  matrix products: 24.9 us -> 0 us
  local copies, waits for them, and re-layouts: 11 us -> 6.45 us
    pallas_call x3 -> x2, Pallas kernels: 276 us -> 242 us  [call(): pl.pallas_call(kernel, out_shape=outs, in_specs=in_specs or [VMEM] * len(...]
    dot_general x10 -> x0, matrix products: 24.9 us -> none  [the longest x1 4.77 us: per_device(): jnp.einsum('rd,fd->rf', expert_rows, w_gate, preferred_element_type=F32)]
where the time goes in v2:
time: 255 us
  Pallas kernels  242 us (95%)
  local copies, waits for them, and re-layouts  6.45 us (3%)
  other arithmetic  5.95 us (2%)
    pallas_call x2, Pallas kernels, call(): pl.pallas_call(kernel, out_shape=outs, in_specs=in_specs or [VMEM] * len(...  242 us
    unnamed x5, local copies, waits for them, and re-layouts  5.58 us

profile of v2, /device:TPU:1, one launch (start us, length us, event | category | flops | bytes accessed | tf_op | source)
XLA Modules:
  0.0 254.9 jit_solution(18215921358936744042)
XLA Ops:
  0.6 0.1 fusion.33
  0.7 0.1 pad.2.clone
  0.8 0.7 convert_bitcast_fusion
  1.5 1.3 maximum_maximum_fusion.small
  2.8 1.3 pad_maximum_fusion.mod
  4.1 0.8 broadcast_in_dim.13.want
  4.9 157.5 %shard_map.156 = (bf16[4,16,24,2048]{3,2,1,0:T(8,128)(2,1)}, bf16[4,16,24,2048]{3,2,1,0:T(8,128)(2,1)}, f32[128,2048]{1,0:T(8,128)}, bf16[512,384]{1,0:T(8,128)(2,1)}, bf16[512,384]{1,0:T(8,128)(2,1)}) custom-call(bf16[128,1024]{1,0:T(8,128)(2,1)} %bitcast.20, bf16[128,1024]{1,0:T(8,128)(2,1)} %bitcast.21, bf16[1024,2048]{1,0:T(8,128)(2,1)} %out_proj.1, ...), custom_call_target="tpu_custom_call" | custom-call | tf_op jit(solution)/shard_map/pallas_call | solution.py:524
  162.5 84.3 %shard_map.157 = (f32[128,2048]{1,0:T(8,128)}, bf16[256,2048]{1,0:T(8,128)(2,1)}, bf16[256,2048]{1,0:T(8,128)(2,1)}, bf16[256,2048]{1,0:T(8,128)(2,1)}) custom-call(bf16[1536,2048]{1,0:T(8,128)(2,1)} %bitcast.17, bf16[1536,2048]{1,0:T(8,128)(2,1)} %bitcast.16, bf16[256,2048]{1,0:T(8,128)(2,1)} %w_gate.1, bf16[256,2048]{1,0:T(8,128)(2,1)} %w_up.1, ...), custom_call_target="tpu_custom_call" | custom-call | tf_op jit(solution)/shard_map/pallas_call | solution.py:524
  246.8 0.0 copy-start
  246.8 2.5 fusion
  249.3 2.3 copy.20
  251.6 2.3 copy.21
  253.9 0.0 copy-done
  253.9 1.0 copy.22
  (1 shorter events, 0.0 us)
Async XLA Ops:
  246.8 7.2 %copy-start = (bf16[256,2048]{1,0:T(8,128)(2,1)S(1)}, bf16[256,2048]{1,0:T(8,128)(2,1)}, u32[]{:S(2)}) copy-start(bf16[256,2048]{1,0:T(8,128)(2,1)} %get-tuple-element.29) | copy-start | bytes 3145732

commit v3 on v2

--- a/solution.py
+++ b/solution.py
@@ -12,6 +12,7 @@
 YN = 4
 MSGS = 16
 ROWS = YN * CAP
+LAG = 3
 MESH = pl.DeviceIdType.MESH
 BF = jnp.bfloat16
 F32 = jnp.float32
@@ -32,22 +33,20 @@
 
 
 def offset(k):
-    t = lax.div(k, 2)
-    odd = lax.rem(t, 2)
-    dz = odd * lax.div(t + 1, 2) + (1 - odd) * lax.rem(8 - lax.div(t, 2), 8)
-    return dz, lax.rem(k, 2)
+    t = lax.rem(k, 4)
+    return 2 * (t + lax.div(t, 2) * (1 - 2 * lax.rem(t, 2))), lax.div(k, 4)
 
 
 def dest(k):
     z, y, x, core = coords()
-    dz, a = offset(k)
-    return dev(lax.rem(z + dz, 8), y, x + a * (3 - 2 * x), core)
+    dz, dy = offset(k)
+    return dev(lax.rem(z + dz, 8), lax.rem(y + dy, 4), x + core * (3 - 2 * x), 1 - core)
 
 
 def source(k):
     z, y, x, core = coords()
-    dz, a = offset(k)
-    return dev(lax.rem(z + 8 - dz, 8), y, x + a * (3 - 2 * x), core)
+    dz, dy = offset(k)
+    return dev(lax.rem(z + 8 - dz, 8), lax.rem(y + 4 - dy, 4), x + (1 - core) * (3 - 2 * x), 1 - core)
 
 
 def core_mate():
@@ -65,6 +64,11 @@
     return dev(z + 1 - 2 * lax.rem(z, 2), y, x, core)
 
 
+def diagonal():
+    z, y, x, core = coords()
+    return dev(z + 1 - 2 * lax.rem(z, 2), y, x, 1 - core)
+
+
 def y_peer(step):
     z, y, x, core = coords()
     return dev(z, lax.rem(y + step, 4), x, core)
@@ -78,10 +82,17 @@
 
     greet(core_mate())
     greet(x_mate())
-    for step in (1, 2, 3):
-        greet(y_peer(step))
-    lax.fori_loop(1, MSGS, lambda k, s: (greet(dest(k)), s)[1], 0)
-    pl.semaphore_wait(barrier, 5 + MSGS - 1)
+    greet(z_mate())
+    greet(diagonal())
+    greet(y_peer(1))
+    greet(y_peer(3))
+
+    def far(k):
+        greet(dest(k))
+        greet(source(k))
+
+    each(0, MSGS, far)
+    pl.semaphore_wait(barrier, 6 + 2 * MSGS)
 
 
 def remote(src, dst, send, recv, device):
@@ -99,50 +110,50 @@
 
 
 class Dispatch:
-    def __init__(self, src, out, cols, send, recv, local):
-        self.src, self.out, self.cols = src, out, cols
+    def __init__(self, src, out, send, recv):
+        self.src, self.out = src, out
         self.send, self.recv = send, recv
-        self.local = pltpu.make_async_copy(src.at[0, :, cols], out.at[0, 0, :, cols], local)
 
     def hop(self, stage, src, block, k, device):
         return remote(
-            src, self.out.at[block, k, :, self.cols], self.send.at[stage, k], self.recv.at[stage, k], device
+            src, self.out.at[block, k], self.send.at[stage, k], self.recv.at[stage, k], device
         )
 
     def first(self, k):
-        return self.hop(0, self.src.at[k, :, self.cols], 0, k, dest(k))
+        return self.hop(0, self.src.at[k], 0, k, dest(k))
 
     def to_core(self, k):
-        return self.hop(1, self.out.at[0, k, :, self.cols], 1, k, core_mate())
+        return self.hop(1, self.out.at[0, k], 1, k, core_mate())
 
     def to_x(self, k):
-        return self.hop(2, self.out.at[0, k, :, self.cols], 2, k, x_mate())
+        return self.hop(2, self.out.at[0, k], 2, k, x_mate())
 
     def onward(self, k):
-        return self.hop(3, self.out.at[2, k, :, self.cols], 3, k, core_mate())
+        return self.hop(3, self.out.at[2, k], 3, k, core_mate())
 
     def start(self):
-        self.local.start()
-        each(1, MSGS, lambda k: self.first(k).start())
-
-    def spread_own(self):
-        self.local.wait()
-        self.to_core(0).start()
-        self.to_x(0).start()
+        each(0, MSGS, lambda k: self.first(k).start())
+
+    def arrive(self, k):
+        self.first(k).wait_recv()
+        self.to_core(k).start()
+        self.to_x(k).start()
+
+    def pass_on(self, k):
+        self.to_x(k).wait_recv()
+        self.onward(k).start()
+
+    def step(self, k):
+        self.arrive(k)
+        self.pass_on(k - LAG)
 
     def spread(self, lower, upper):
-        def step(k):
-            self.first(k).wait_recv()
-            self.to_core(k).start()
-            self.to_x(k).start()
-            self.to_x(k - 1).wait_recv()
-            self.onward(k - 1).start()
-
-        each(lower, upper, step)
+        for k in range(lower, min(upper, LAG)):
+            self.arrive(k)
+        each(max(lower, LAG), upper, self.step)
 
     def spread_last(self):
-        self.to_x(MSGS - 1).wait_recv()
-        self.onward(MSGS - 1).start()
+        each(MSGS - LAG, MSGS, self.pass_on)
 
     def finish(self):
         def step(k):
@@ -152,8 +163,9 @@
             self.to_x(k).wait_send()
             self.onward(k).wait_send()
 
+            self.first(k).wait_send()
+
         each(0, MSGS, step)
-        each(1, MSGS, lambda k: self.first(k).wait_send())
 
 
 class Ring:
@@ -182,22 +194,30 @@
             copy.wait_send()
 
 
-def row_ring(src, buf, cols, send, recv):
-    n = src.shape[0]
-    half = n // 2
-
-    def piece(block, h):
-        return buf.at[pl.ds(block * n + h * half, half), cols]
-
-    return Ring(
-        src.at[:, cols],
-        piece,
-        buf.at[pl.ds(n, n), cols],
-        buf.at[pl.ds(2 * n, n), cols],
-        lambda h: piece(3, h),
-        send,
-        recv,
-    )
+class Quad:
+    def __init__(self, src, buf, send, recv):
+        n = src.shape[0]
+        self.mate = remote(src, buf.at[pl.ds(n, n)], send.at[0], recv.at[0], core_mate())
+        self.zed = remote(src, buf.at[pl.ds(2 * n, n)], send.at[1], recv.at[1], z_mate())
+        self.far = remote(
+            buf.at[pl.ds(2 * n, n)], buf.at[pl.ds(3 * n, n)], send.at[2], recv.at[2], core_mate()
+        )
+
+    def start(self):
+        self.zed.start()
+        self.mate.start()
+
+    def middle(self):
+        self.zed.wait_recv()
+        self.far.start()
+
+    def finish(self):
+        self.mate.wait_recv()
+        self.far.wait_recv()
+
+    def drain(self):
+        for copy in (self.mate, self.zed, self.far):
+            copy.wait_send()
 
 
 def kv_ring(buf, base, send, recv):
@@ -212,18 +232,18 @@
     )
 
 
-def place(chooser, tokens, scale, placed, base, size):
+def place(chooser, tokens, scale, placed):
     width = 512
 
     def step(j):
-        cols = pl.ds(pl.multiple_of(base + j * width, width), width)
+        cols = pl.ds(pl.multiple_of(j * width, width), width)
         rows = jnp.dot(chooser[...], tokens[:, cols], preferred_element_type=F32)
         if scale is not None:
             rows = rows * scale[...]
         for k in range(MSGS):
             placed[k, :, cols] = rows[k * ROWS : (k + 1) * ROWS].astype(BF)
 
-    each(0, size // width, step)
+    each(0, tokens.shape[1] // width, step)
 
 
 def attend(queries, kvall, attended, h):
@@ -239,17 +259,13 @@
     attended[:, cols] = (mixed / total).astype(BF)
 
 
-CHUNKS = 1
-
-
 def forward_kernel(
     keys, values, out_proj, og, queries, tokens, mod, small, want,
     cot, expert_in, mixed, hi, lo,
     kvall, ogall, nall, smallall, ready, scale, placed_cot, placed_in, chooser, attended, normed, proj,
-    load, local, kv_s, kv_r, og_s, og_r, small_s, small_r, n_s, n_r, c_s, c_r, d_s, d_r,
+    load, kv_s, kv_r, og_s, og_r, small_s, small_r, n_s, n_r, c_s, c_r, d_s, d_r,
 ):
     n, width = og.shape
-    every = pl.ds(0, width)
     key_load = pltpu.make_async_copy(keys, kvall.at[0, 0], load.at[0])
     value_load = pltpu.make_async_copy(values, kvall.at[0, 1], load.at[1])
     proj_load = pltpu.make_async_copy(out_proj, proj, load.at[2])
@@ -268,34 +284,30 @@
     ready[1:2, :] = small[1:2, :] * CAP + slot1
     ready[2:8, :] = small[2:8, :]
     enter()
-    og_ring = row_ring(og, ogall, every, og_s, og_r)
-    og_ring.start()
-    key_load.wait()
-    value_load.wait()
-    zed = remote(kvall.at[0], kvall.at[4], kv_s.at[0, 4], kv_r.at[0, 4], z_mate())
-    zed.start()
-    near = kv_ring(kvall, 0, kv_s.at[0], kv_r.at[0])
-    near.start()
     small_sends = [
-        remote(ready, smallall.at[step], small_s.at[step - 1], small_r.at[step - 1], y_peer(step))
-        for step in (1, 2, 3)
+        remote(ready, smallall.at[s], small_s.at[s - 1], small_r.at[s - 1], device)
+        for s, device in ((1, core_mate()), (2, z_mate()), (3, diagonal()))
     ]
     for copy in small_sends:
         copy.start()
+    og_quad = Quad(og, ogall, og_s, og_r)
+    og_quad.start()
+    key_load.wait()
+    value_load.wait()
+    near = kv_ring(kvall, 0, kv_s.at[0], kv_r.at[0])
+    near.start()
+    zed = remote(kvall.at[0], kvall.at[4], kv_s.at[0, 4], kv_r.at[0, 4], z_mate())
+    zed.start()
     ogall[0:n] = og[...]
     smallall[0] = ready[...]
-    og_ring.middle()
-    zed.wait_recv()
-    other = kv_ring(kvall, 4, kv_s.at[1], kv_r.at[1])
-    other.start()
     for copy in small_sends:
         copy.wait_recv()
     total = jnp.zeros((MSGS * ROWS, 1), F32)
-    for block, slot in ((0, 0), (1, 1), (2, 3), (3, 2)):
+    for block in range(4):
         shift = float(block * 64 * CAP)
-        hit0 = want[...] == smallall[slot, 0:1, :] + shift
-        hit1 = want[...] == smallall[slot, 1:2, :] + shift
-        gate = jnp.where(hit0, smallall[slot, 2:3, :], 0.0) + jnp.where(hit1, smallall[slot, 3:4, :], 0.0)
+        hit0 = want[...] == smallall[block, 0:1, :] + shift
+        hit1 = want[...] == smallall[block, 1:2, :] + shift
+        gate = jnp.where(hit0, smallall[block, 2:3, :], 0.0) + jnp.where(hit1, smallall[block, 3:4, :], 0.0)
         picks = jnp.where(hit0, 1.0, 0.0) + jnp.where(hit1, 1.0, 0.0)
         chooser[:, block * n : (block + 1) * n] = picks.astype(BF)
         turned = gate.T
@@ -304,20 +316,26 @@
         lo[block * n : (block + 1) * n, :] = (turned - top.astype(F32)).astype(BF)
         total = total + jnp.sum(gate, axis=1, keepdims=True)
     scale[...] = total
+    og_quad.middle()
     near.middle()
-    og_ring.finish()
-    place(chooser, ogall, scale, placed_cot, 0, width)
-    cot_sends = Dispatch(placed_cot, cot, every, c_s, c_r, local.at[0])
+    og_quad.finish()
+    place(chooser, ogall, scale, placed_cot)
+    cot_sends = Dispatch(placed_cot, cot, c_s, c_r)
     cot_sends.start()
+    zed.wait_recv()
+    other = kv_ring(kvall, 4, kv_s.at[1], kv_r.at[1])
+    other.start()
+    cot_sends.spread(0, 2)
     other.middle()
-    cot_sends.spread_own()
-    cot_sends.spread(1, 5)
+    cot_sends.spread(2, 5)
     near.finish()
     other.finish()
-    each(0, HEADS // 2, lambda h: attend(queries, kvall, attended, h))
-    cot_sends.spread(5, 10)
-    each(HEADS // 2, HEADS, lambda h: attend(queries, kvall, attended, h))
-    cot_sends.spread(10, 14)
+
+    def attend_and_spread(h):
+        attend(queries, kvall, attended, h)
+        cot_sends.step(h + 5)
+
+    each(0, HEADS, attend_and_spread)
     proj_load.wait()
     part = 512
     squares = jnp.zeros((n, 1), F32)
@@ -329,36 +347,23 @@
         mixed[:, cols] = value
         squares = squares + jnp.sum(value * value, axis=1, keepdims=True)
     inverse = lax.rsqrt(squares * (1.0 / width) + 1e-06)
-    size = width // CHUNKS
-    rings, sends = [], []
-    for chunk in range(CHUNKS):
-        cols = pl.ds(chunk * size, size)
-        window = slice(chunk * size, (chunk + 1) * size)
-        normed[:, window] = (
-            mixed[:, window] * inverse * (1.0 + mod[0:1, window]) + mod[1:2, window]
-        ).astype(BF)
-        ring = row_ring(normed, nall, cols, n_s.at[chunk], n_r.at[chunk])
-        ring.start()
-        rings.append(ring)
-        sends.append(Dispatch(placed_in, expert_in, cols, d_s.at[chunk], d_r.at[chunk], local.at[1 + chunk]))
+    normed[...] = (mixed[...] * inverse * (1.0 + mod[0:1, :]) + mod[1:2, :]).astype(BF)
+    quad = Quad(normed, nall, n_s, n_r)
+    quad.start()
     nall[0:n] = normed[...]
-    cot_sends.spread(14, 16)
+    cot_sends.spread(13, 16)
     cot_sends.spread_last()
-    for ring in rings:
-        ring.middle()
-    for chunk in range(CHUNKS):
-        rings[chunk].finish()
-        place(chooser, nall, None, placed_in, chunk * size, size)
-        sends[chunk].start()
-    for chunk in range(CHUNKS):
-        sends[chunk].spread_own()
-        sends[chunk].spread(1, MSGS)
-        sends[chunk].spread_last()
+    quad.middle()
+    quad.finish()
+    place(chooser, nall, None, placed_in)
+    sends = Dispatch(placed_in, expert_in, d_s, d_r)
+    sends.start()
+    sends.spread(0, MSGS)
+    sends.spread_last()
     cot_sends.finish()
-    for chunk in range(CHUNKS):
-        sends[chunk].finish()
-        rings[chunk].drain()
-    og_ring.drain()
+    sends.finish()
+    quad.drain()
+    og_quad.drain()
     near.drain()
     other.drain()
     zed.wait_send()
@@ -373,7 +378,7 @@
     rows_in, cots_in, w_gate, w_up, w_down, hi, lo,
     out, grad_gate, grad_up, grad_down,
     rows, cots, gate, up, hidden_t, gate_t, up_t,
-    pieces, from_core, from_diag, pair, from_x, summed, back, flat, partial, peers,
+    pieces, from_core, from_diag, pair, from_x, summed, back, flat, middle, partial, peers,
     load, c_s, c_r, b_s, b_r, p_s, p_r,
 ):
     block_rows = MSGS * ROWS
@@ -458,13 +463,11 @@
             value = pieces[c, 0, k].astype(F32) + from_core[c, k].astype(F32) + from_x[c, k].astype(F32)
             return value.astype(BF)
 
-        flat[0:ROWS, cols] = total(0).astype(F32)
-
         def send_home(k):
             summed[c, k] = total(k)
             home(c, k).start()
 
-        each(1, MSGS, send_home)
+        each(0, MSGS, send_home)
 
     def gradients(j):
         cols = pl.ds(pl.multiple_of(j * part, part), part)
@@ -474,11 +477,10 @@
 
     each(0, width // part, gradients)
 
-    steps = {1: 3, 2: 1, 3: 2}
-
     def to_peer(c, block):
         b = block - 1
-        return remote(partial.at[c, b], peers.at[c, b], p_s.at[c, b], p_r.at[c, b], y_peer(steps[block]))
+        device = z_mate() if block == 2 else core_mate()
+        return remote(partial.at[c, b], peers.at[c, b], p_s.at[c, b], p_r.at[c, b], device)
 
     for c in range(PARTS):
         cols = slice(c * size, (c + 1) * size)
@@ -487,8 +489,8 @@
             home(c, k).wait_recv()
             flat[pl.ds(pl.multiple_of(k * ROWS, 8), ROWS), cols] = back[c, k].astype(F32)
 
-        each(1, MSGS, take)
-        for block in (3, 1, 2, 0):
+        each(0, MSGS, take)
+        for block in (3, 2, 1, 0):
             mine = slice(block * n, (block + 1) * n)
             for j in range(size // part):
                 at = c * size + j * part
@@ -496,15 +498,22 @@
                 value = jnp.dot(hi[mine], values, preferred_element_type=F32) + jnp.dot(
                     lo[mine], values, preferred_element_type=F32
                 )
-                if block:
-                    partial[c, block - 1, :, j * part : (j + 1) * part] = value.astype(BF)
+                here = slice(j * part, (j + 1) * part)
+                if block == 2:
+                    middle[c, :, here] = value
+                elif block:
+                    partial[c, block - 1, :, here] = value.astype(BF)
                 else:
                     out[:, at : at + part] = value
-            if block:
+            if block == 3 or block == 1:
                 to_peer(c, block).start()
+            if block == 1:
+                to_peer(c, 3).wait_recv()
+                partial[c, 1] = (middle[c] + peers[c, 2].astype(F32)).astype(BF)
+                to_peer(c, 2).start()
     for c in range(PARTS):
         cols = slice(c * size, (c + 1) * size)
-        for block in (1, 2, 3):
+        for block in (1, 2):
             to_peer(c, block).wait_recv()
             out[:, cols] += peers[c, block - 1].astype(F32)
     for c in range(PARTS):
@@ -515,9 +524,16 @@
             mate_diag(c, k).wait_send()
             mate_own(c, k).wait_send()
             across(c, k).wait_send()
+            home(c, k).wait_send()
 
         each(0, MSGS, drain)
-        each(1, MSGS, lambda k: home(c, k).wait_send())
+
+
+def finish_kernel(mixed, combined, a, b, c, out, a_out, b_out, c_out):
+    out[...] = (mixed[...] + combined[...]).astype(BF)
+    a_out[...] = a[...]
+    b_out[...] = b[...]
+    c_out[...] = c[...]
 
 
 def call(kernel, number, outs, scratch, args, in_specs=None, out_specs=None):
@@ -552,15 +568,15 @@
     width = tokens.shape[2]
     inner = queries.shape[2]
     rows = MSGS * ROWS
-    z, y, x, _ = coords()
+    z, y, x, core = coords()
     small = jnp.concatenate(
         [expert_ids[0].T.astype(F32), gates[0].T, jnp.zeros((4, n), F32)], axis=0
     )
     row = jnp.arange(rows, dtype=jnp.int32)
-    dz, a = offset(row // ROWS)
+    dz, dy = offset(row // ROWS)
     to_z = (z + dz) % 8
-    to_x = x + a * (3 - 2 * x)
-    expert = ((to_z % 2) * 4 + y) * 8 + (to_z // 2) * 2 + to_x // 2
+    to_x = x + core * (3 - 2 * x)
+    expert = ((to_z % 2) * 4 + (y + dy) % 4) * 8 + (to_z // 2) * 2 + to_x // 2
     want = (row % ROWS // CAP) * (64 * CAP) + expert * CAP + row % CAP
     want = jnp.broadcast_to(want.astype(F32)[:, None], (rows, n))
     mod = jnp.concatenate([mod_scale, mod_shift], axis=0)
@@ -585,19 +601,18 @@
             pltpu.VMEM((n, width), BF),
             pltpu.VMEM((inner, width), BF),
             DMA((3,)),
-            DMA((1 + CHUNKS,)),
             DMA((2, 5)),
             DMA((2, 5)),
-            DMA((4,)),
-            DMA((4,)),
             DMA((3,)),
             DMA((3,)),
-            DMA((CHUNKS, 4)),
-            DMA((CHUNKS, 4)),
+            DMA((3,)),
+            DMA((3,)),
+            DMA((3,)),
+            DMA((3,)),
             DMA((4, MSGS)),
             DMA((4, MSGS)),
-            DMA((CHUNKS, 4, MSGS)),
-            DMA((CHUNKS, 4, MSGS)),
+            DMA((4, MSGS)),
+            DMA((4, MSGS)),
         ],
         (keys[0], values[0], out_proj, out_grad[0], queries[0], tokens[0], mod, small, want),
         in_specs=[ANY] * 3 + [VMEM] * 6,
@@ -628,6 +643,7 @@
             block,
             block,
             pltpu.VMEM((rows, width), F32),
+            pltpu.VMEM((PARTS, n, width // PARTS), F32),
             share,
             share,
             DMA((5,)),
@@ -641,8 +657,17 @@
         (expert_in.reshape(everything, width), cot.reshape(everything, width), w_gate, w_up, w_down, hi, lo),
         in_specs=[ANY] * 2 + [VMEM] * 5,
     )
-    layer_out = (mixed + combined).astype(BF)[None]
-    return (layer_out, grad_gate, grad_up, grad_down)
+    steps = 4
+    thin = pl.BlockSpec((n // steps, width), lambda i: (i, 0))
+    thick = pl.BlockSpec((hid // steps, width), lambda i: (i, 0))
+    layer_out, grad_gate, grad_up, grad_down = pl.pallas_call(
+        finish_kernel,
+        grid=(steps,),
+        in_specs=[thin, thin, thick, thick, thick],
+        out_specs=(thin, thick, thick, thick),
+        out_shape=(jax.ShapeDtypeStruct((n, width), BF), grad, grad, grad),
+    )(mixed, combined, grad_gate, grad_up, grad_down)
+    return (layer_out[None], grad_gate, grad_up, grad_down)
 
 
 def solution(mesh):

time: 255 us -> 242 us (0.949)
  Pallas kernels: 242 us -> 236 us
  local copies, waits for them, and re-layouts: 6.45 us -> 0.87 us
    pallas_call x2, Pallas kernels: 242 us -> 232 us  [call(): pl.pallas_call(kernel, out_shape=outs, in_specs=in_specs or [VMEM] * len(...]
    unnamed x5 -> x0, local copies, waits for them, and re-layouts: 5.58 us -> none
    pallas_call x0 -> x1, Pallas kernels: none -> 4.75 us  [per_device(): pl.pallas_call(finish_kernel, grid=(steps,), in_specs=[thin, thin, thick,...]
where the time goes in v3:
time: 242 us; the launch traced here: 241 us
  Pallas kernels  236 us (98%)
  other arithmetic  3.41 us (1%)
    pallas_call x2, Pallas kernels, call(): pl.pallas_call(kernel, out_shape=outs, in_specs=in_specs or [VMEM] * len(...  232 us

profile of v3, /device:TPU:1, one launch (start us, length us, event | category | flops | bytes accessed | tf_op | source)
XLA Modules:
  0.0 241.3 jit_solution(5752632404316224621)
XLA Ops:
  0.7 0.1 pad.2.clone
  0.8 0.7 convert_bitcast_fusion
  1.5 1.3 maximum_maximum_fusion.small
  2.8 1.3 pad_maximum_fusion.mod
  4.2 0.8 broadcast_in_dim.13.want
  5.0 156.5 %shard_map.156 = (bf16[4,16,24,2048]{3,2,1,0:T(8,128)(2,1)}, bf16[4,16,24,2048]{3,2,1,0:T(8,128)(2,1)}, f32[128,2048]{1,0:T(8,128)}, bf16[512,384]{1,0:T(8,128)(2,1)}, bf16[512,384]{1,0:T(8,128)(2,1)}) custom-call(bf16[128,1024]{1,0:T(8,128)(2,1)} %bitcast.19, bf16[128,1024]{1,0:T(8,128)(2,1)} %bitcast.20, bf16[1024,2048]{1,0:T(8,128)(2,1)} %out_proj.1, ...), custom_call_target="tpu_custom_call" | custom-call | tf_op jit(solution)/shard_map/pallas_call | solution.py:540
  161.5 75.0 %shard_map.157 = (f32[128,2048]{1,0:T(8,128)}, bf16[256,2048]{1,0:T(8,128)(2,1)}, bf16[256,2048]{1,0:T(8,128)(2,1)}, bf16[256,2048]{1,0:T(8,128)(2,1)}) custom-call(bf16[1536,2048]{1,0:T(8,128)(2,1)} %bitcast.16, bf16[1536,2048]{1,0:T(8,128)(2,1)} %bitcast.15, bf16[256,2048]{1,0:T(8,128)(2,1)} %w_gate.1, bf16[256,2048]{1,0:T(8,128)(2,1)} %w_up.1, ...), custom_call_target="tpu_custom_call" | custom-call | tf_op jit(solution)/shard_map/pallas_call | solution.py:540
  236.6 4.8 %shard_map.158 = (bf16[128,2048]{1,0:T(8,128)(2,1)}, bf16[256,2048]{1,0:T(8,128)(2,1)}, bf16[256,2048]{1,0:T(8,128)(2,1)}, bf16[256,2048]{1,0:T(8,128)(2,1)}) custom-call(f32[128,2048]{1,0:T(8,128)} %get-tuple-element.17.mixed, f32[128,2048]{1,0:T(8,128)} %get-tuple-element.22.combined, bf16[256,2048]{1,0:T(8,128)(2,1)} %get-tuple-element.23.a, ...), custom_call_target="tpu_custom_call" | custom-call | tf_op jit(solution)/shard_map/pallas_call | solution.py:663
  (2 shorter events, 0.1 us)

commit v4 on v3

--- a/solution.py
+++ b/solution.py
@@ -32,21 +32,21 @@
     return {"ctx": lax.rem(z, 2) * 4 + y, "exp": lax.div(z, 2) * 8 + x * 2 + core}
 
 
-def offset(k):
+def offset(k, core):
     t = lax.rem(k, 4)
-    return 2 * (t + lax.div(t, 2) * (1 - 2 * lax.rem(t, 2))), lax.div(k, 4)
+    return 2 * (t + lax.div(t, 2) * (1 - 2 * lax.rem(t, 2))) + core, lax.div(k, 4)
 
 
 def dest(k):
     z, y, x, core = coords()
-    dz, dy = offset(k)
-    return dev(lax.rem(z + dz, 8), lax.rem(y + dy, 4), x + core * (3 - 2 * x), 1 - core)
+    dz, dy = offset(k, core)
+    return dev(lax.rem(z + dz, 8), lax.rem(y + dy, 4), x, 1 - core)
 
 
 def source(k):
     z, y, x, core = coords()
-    dz, dy = offset(k)
-    return dev(lax.rem(z + 8 - dz, 8), lax.rem(y + 4 - dy, 4), x + (1 - core) * (3 - 2 * x), 1 - core)
+    dz, dy = offset(k, 1 - core)
+    return dev(lax.rem(z + 8 - dz, 8), lax.rem(y + 4 - dy, 4), x, 1 - core)
 
 
 def core_mate():
@@ -64,9 +64,14 @@
     return dev(z + 1 - 2 * lax.rem(z, 2), y, x, core)
 
 
+def flip_mate():
+    z, y, x, core = coords()
+    return dev(z, y, 3 - x, core)
+
+
 def diagonal():
     z, y, x, core = coords()
-    return dev(z + 1 - 2 * lax.rem(z, 2), y, x, 1 - core)
+    return dev(z, y, 3 - x, 1 - core)
 
 
 def y_peer(step):
@@ -83,6 +88,7 @@
     greet(core_mate())
     greet(x_mate())
     greet(z_mate())
+    greet(flip_mate())
     greet(diagonal())
     greet(y_peer(1))
     greet(y_peer(3))
@@ -92,7 +98,7 @@
         greet(source(k))
 
     each(0, MSGS, far)
-    pl.semaphore_wait(barrier, 6 + 2 * MSGS)
+    pl.semaphore_wait(barrier, 7 + 2 * MSGS)
 
 
 def remote(src, dst, send, recv, device):
@@ -198,17 +204,17 @@
     def __init__(self, src, buf, send, recv):
         n = src.shape[0]
         self.mate = remote(src, buf.at[pl.ds(n, n)], send.at[0], recv.at[0], core_mate())
-        self.zed = remote(src, buf.at[pl.ds(2 * n, n)], send.at[1], recv.at[1], z_mate())
+        self.flip = remote(src, buf.at[pl.ds(2 * n, n)], send.at[1], recv.at[1], flip_mate())
         self.far = remote(
             buf.at[pl.ds(2 * n, n)], buf.at[pl.ds(3 * n, n)], send.at[2], recv.at[2], core_mate()
         )
 
     def start(self):
-        self.zed.start()
+        self.flip.start()
         self.mate.start()
 
     def middle(self):
-        self.zed.wait_recv()
+        self.flip.wait_recv()
         self.far.start()
 
     def finish(self):
@@ -216,7 +222,7 @@
         self.far.wait_recv()
 
     def drain(self):
-        for copy in (self.mate, self.zed, self.far):
+        for copy in (self.mate, self.flip, self.far):
             copy.wait_send()
 
 
@@ -260,7 +266,7 @@
 
 
 def forward_kernel(
-    keys, values, out_proj, og, queries, tokens, mod, small, want,
+    keys, values, out_proj, og, queries, tokens, mod_scale, mod_shift, small, want,
     cot, expert_in, mixed, hi, lo,
     kvall, ogall, nall, smallall, ready, scale, placed_cot, placed_in, chooser, attended, normed, proj,
     load, kv_s, kv_r, og_s, og_r, small_s, small_r, n_s, n_r, c_s, c_r, d_s, d_r,
@@ -286,7 +292,7 @@
     enter()
     small_sends = [
         remote(ready, smallall.at[s], small_s.at[s - 1], small_r.at[s - 1], device)
-        for s, device in ((1, core_mate()), (2, z_mate()), (3, diagonal()))
+        for s, device in ((1, core_mate()), (2, flip_mate()), (3, diagonal()))
     ]
     for copy in small_sends:
         copy.start()
@@ -294,10 +300,10 @@
     og_quad.start()
     key_load.wait()
     value_load.wait()
+    zed = remote(kvall.at[0], kvall.at[4], kv_s.at[0, 4], kv_r.at[0, 4], z_mate())
+    zed.start()
     near = kv_ring(kvall, 0, kv_s.at[0], kv_r.at[0])
     near.start()
-    zed = remote(kvall.at[0], kvall.at[4], kv_s.at[0, 4], kv_r.at[0, 4], z_mate())
-    zed.start()
     ogall[0:n] = og[...]
     smallall[0] = ready[...]
     for copy in small_sends:
@@ -317,14 +323,14 @@
         total = total + jnp.sum(gate, axis=1, keepdims=True)
     scale[...] = total
     og_quad.middle()
+    zed.wait_recv()
+    other = kv_ring(kvall, 4, kv_s.at[1], kv_r.at[1])
+    other.start()
     near.middle()
     og_quad.finish()
     place(chooser, ogall, scale, placed_cot)
     cot_sends = Dispatch(placed_cot, cot, c_s, c_r)
     cot_sends.start()
-    zed.wait_recv()
-    other = kv_ring(kvall, 4, kv_s.at[1], kv_r.at[1])
-    other.start()
     cot_sends.spread(0, 2)
     other.middle()
     cot_sends.spread(2, 5)
@@ -347,7 +353,7 @@
         mixed[:, cols] = value
         squares = squares + jnp.sum(value * value, axis=1, keepdims=True)
     inverse = lax.rsqrt(squares * (1.0 / width) + 1e-06)
-    normed[...] = (mixed[...] * inverse * (1.0 + mod[0:1, :]) + mod[1:2, :]).astype(BF)
+    normed[...] = (mixed[...] * inverse * (1.0 + mod_scale[...]) + mod_shift[...]).astype(BF)
     quad = Quad(normed, nall, n_s, n_r)
     quad.start()
     nall[0:n] = normed[...]
@@ -479,7 +485,7 @@
 
     def to_peer(c, block):
         b = block - 1
-        device = z_mate() if block == 2 else core_mate()
+        device = flip_mate() if block == 2 else core_mate()
         return remote(partial.at[c, b], peers.at[c, b], p_s.at[c, b], p_r.at[c, b], device)
 
     for c in range(PARTS):
@@ -573,13 +579,11 @@
         [expert_ids[0].T.astype(F32), gates[0].T, jnp.zeros((4, n), F32)], axis=0
     )
     row = jnp.arange(rows, dtype=jnp.int32)
-    dz, dy = offset(row // ROWS)
+    dz, dy = offset(row // ROWS, core)
     to_z = (z + dz) % 8
-    to_x = x + core * (3 - 2 * x)
-    expert = ((to_z % 2) * 4 + (y + dy) % 4) * 8 + (to_z // 2) * 2 + to_x // 2
+    expert = ((to_z % 2) * 4 + (y + dy) % 4) * 8 + (to_z // 2) * 2 + x // 2
     want = (row % ROWS // CAP) * (64 * CAP) + expert * CAP + row % CAP
     want = jnp.broadcast_to(want.astype(F32)[:, None], (rows, n))
-    mod = jnp.concatenate([mod_scale, mod_shift], axis=0)
 
     slots = jax.ShapeDtypeStruct((4, MSGS, ROWS, width), BF)
     routed = jax.ShapeDtypeStruct((YN * n, rows), BF)
@@ -614,8 +618,8 @@
             DMA((4, MSGS)),
             DMA((4, MSGS)),
         ],
-        (keys[0], values[0], out_proj, out_grad[0], queries[0], tokens[0], mod, small, want),
-        in_specs=[ANY] * 3 + [VMEM] * 6,
+        (keys[0], values[0], out_proj, out_grad[0], queries[0], tokens[0], mod_scale, mod_shift, small, want),
+        in_specs=[ANY] * 3 + [VMEM] * 7,
         out_specs=(ANY, ANY, VMEM, VMEM, VMEM),
     )
     everything = 4 * rows

time: 242 us -> 229 us (0.946)
  Pallas kernels: 236 us -> 226 us
    pallas_call x2, Pallas kernels: 232 us -> 221 us  [call(): pl.pallas_call(kernel, out_shape=outs, in_specs=in_specs or [VMEM] * len(...]
where the time goes in v4:
time: 229 us
  Pallas kernels  226 us (99%)
    pallas_call x2, Pallas kernels, call(): pl.pallas_call(kernel, out_shape=outs, in_specs=in_specs or [VMEM] * len(...  221 us
    pallas_call x1, Pallas kernels, per_device(): pl.pallas_call(finish_kernel, grid=(steps,), in_specs=[thin, thin, thick,...  4.75 us

profile of v4, /device:TPU:1, one launch (start us, length us, event | category | flops | bytes accessed | tf_op | source)
XLA Modules:
  0.0 229.2 jit_solution(7611066037770700403)
XLA Ops:
  0.7 0.1 fusion.30
  0.7 0.1 pad.2.clone
  0.8 0.7 convert_bitcast_fusion
  1.5 1.3 maximum_maximum_fusion.small
  2.8 0.8 broadcast_in_dim.13.want
  3.6 145.3 %shard_map.156 = (bf16[4,16,24,2048]{3,2,1,0:T(8,128)(2,1)}, bf16[4,16,24,2048]{3,2,1,0:T(8,128)(2,1)}, f32[128,2048]{1,0:T(8,128)}, bf16[512,384]{1,0:T(8,128)(2,1)}, bf16[512,384]{1,0:T(8,128)(2,1)}) custom-call(bf16[128,1024]{1,0:T(8,128)(2,1)} %bitcast.19, bf16[128,1024]{1,0:T(8,128)(2,1)} %bitcast.20, bf16[1024,2048]{1,0:T(8,128)(2,1)} %out_proj.1, ...), custom_call_target="tpu_custom_call" | custom-call | tf_op jit(solution)/shard_map/pallas_call | solution.py:546
  149.0 75.4 %shard_map.157 = (f32[128,2048]{1,0:T(8,128)}, bf16[256,2048]{1,0:T(8,128)(2,1)}, bf16[256,2048]{1,0:T(8,128)(2,1)}, bf16[256,2048]{1,0:T(8,128)(2,1)}) custom-call(bf16[1536,2048]{1,0:T(8,128)(2,1)} %bitcast.16, bf16[1536,2048]{1,0:T(8,128)(2,1)} %bitcast.15, bf16[256,2048]{1,0:T(8,128)(2,1)} %w_gate.1, bf16[256,2048]{1,0:T(8,128)(2,1)} %w_up.1, ...), custom_call_target="tpu_custom_call" | custom-call | tf_op jit(solution)/shard_map/pallas_call | solution.py:546
  224.4 4.8 %shard_map.158 = (bf16[128,2048]{1,0:T(8,128)(2,1)}, bf16[256,2048]{1,0:T(8,128)(2,1)}, bf16[256,2048]{1,0:T(8,128)(2,1)}, bf16[256,2048]{1,0:T(8,128)(2,1)}) custom-call(f32[128,2048]{1,0:T(8,128)} %get-tuple-element.17.mixed, f32[128,2048]{1,0:T(8,128)} %get-tuple-element.22.combined, bf16[256,2048]{1,0:T(8,128)(2,1)} %get-tuple-element.23.a, ...), custom_call_target="tpu_custom_call" | custom-call | tf_op jit(solution)/shard_map/pallas_call | solution.py:667
  (1 shorter events, 0.0 us)

commit v5 on v4

--- a/solution.py
+++ b/solution.py
@@ -79,7 +79,7 @@
     return dev(z, lax.rem(y + step, 4), x, core)
 
 
-def enter():
+def hello():
     barrier = pltpu.get_barrier_semaphore()
 
     def greet(device):
@@ -98,7 +98,10 @@
         greet(source(k))
 
     each(0, MSGS, far)
-    pl.semaphore_wait(barrier, 7 + 2 * MSGS)
+
+
+def everyone_here():
+    pl.semaphore_wait(pltpu.get_barrier_semaphore(), 7 + 2 * MSGS)
 
 
 def remote(src, dst, send, recv, device):
@@ -272,6 +275,7 @@
     load, kv_s, kv_r, og_s, og_r, small_s, small_r, n_s, n_r, c_s, c_r, d_s, d_r,
 ):
     n, width = og.shape
+    hello()
     key_load = pltpu.make_async_copy(keys, kvall.at[0, 0], load.at[0])
     value_load = pltpu.make_async_copy(values, kvall.at[0, 1], load.at[1])
     proj_load = pltpu.make_async_copy(out_proj, proj, load.at[2])
@@ -289,7 +293,7 @@
     ready[0:1, :] = small[0:1, :] * CAP + slot0
     ready[1:2, :] = small[1:2, :] * CAP + slot1
     ready[2:8, :] = small[2:8, :]
-    enter()
+    everyone_here()
     small_sends = [
         remote(ready, smallall.at[s], small_s.at[s - 1], small_r.at[s - 1], device)
         for s, device in ((1, core_mate()), (2, flip_mate()), (3, diagonal()))
@@ -404,7 +408,7 @@
     for copy in row_loads:
         copy.start()
     cot_load.start()
-    enter()
+    hello()
 
     def mate_own(c, k):
         return remote(pieces.at[c, 1, k], from_core.at[c, k], c_s.at[c, 0, k], c_r.at[c, 0, k], core_mate())
@@ -435,6 +439,7 @@
             for k in range(MSGS):
                 pieces[c, block, k, :, base : base + part] = value[k * ROWS : (k + 1) * ROWS].astype(BF)
         if block == 3:
+            everyone_here()
             for c in range(PARTS):
                 each(0, MSGS, lambda k: mate_diag(c, k).start())
         if block == 1:

time: 229 us -> 227 us (level)
  Pallas kernels: 226 us -> 223 us
where the time goes in v5:
time: 227 us
  Pallas kernels  223 us (98%)
    pallas_call x2, Pallas kernels, call(): pl.pallas_call(kernel, out_shape=outs, in_specs=in_specs or [VMEM] * len(...  219 us
    pallas_call x1, Pallas kernels, per_device(): pl.pallas_call(finish_kernel, grid=(steps,), in_specs=[thin, thin, thick,...  4.75 us

profile of v5, /device:TPU:1, one launch (start us, length us, event | category | flops | bytes accessed | tf_op | source)
XLA Modules:
  0.0 227.0 jit_solution(3163248793480685462)
XLA Ops:
  0.7 0.1 fusion.30
  0.7 0.1 pad.2.clone
  0.8 0.7 convert_bitcast_fusion
  1.5 1.3 maximum_maximum_fusion.small
  2.8 0.8 broadcast_in_dim.13.want
  3.6 145.0 %shard_map.156 = (bf16[4,16,24,2048]{3,2,1,0:T(8,128)(2,1)}, bf16[4,16,24,2048]{3,2,1,0:T(8,128)(2,1)}, f32[128,2048]{1,0:T(8,128)}, bf16[512,384]{1,0:T(8,128)(2,1)}, bf16[512,384]{1,0:T(8,128)(2,1)}) custom-call(bf16[128,1024]{1,0:T(8,128)(2,1)} %bitcast.19, bf16[128,1024]{1,0:T(8,128)(2,1)} %bitcast.20, bf16[1024,2048]{1,0:T(8,128)(2,1)} %out_proj.1, ...), custom_call_target="tpu_custom_call" | custom-call | tf_op jit(solution)/shard_map/pallas_call | solution.py:551
  148.6 73.6 %shard_map.157 = (f32[128,2048]{1,0:T(8,128)}, bf16[256,2048]{1,0:T(8,128)(2,1)}, bf16[256,2048]{1,0:T(8,128)(2,1)}, bf16[256,2048]{1,0:T(8,128)(2,1)}) custom-call(bf16[1536,2048]{1,0:T(8,128)(2,1)} %bitcast.16, bf16[1536,2048]{1,0:T(8,128)(2,1)} %bitcast.15, bf16[256,2048]{1,0:T(8,128)(2,1)} %w_gate.1, bf16[256,2048]{1,0:T(8,128)(2,1)} %w_up.1, ...), custom_call_target="tpu_custom_call" | custom-call | tf_op jit(solution)/shard_map/pallas_call | solution.py:551
  222.2 4.8 %shard_map.158 = (bf16[128,2048]{1,0:T(8,128)(2,1)}, bf16[256,2048]{1,0:T(8,128)(2,1)}, bf16[256,2048]{1,0:T(8,128)(2,1)}, bf16[256,2048]{1,0:T(8,128)(2,1)}) custom-call(f32[128,2048]{1,0:T(8,128)} %get-tuple-element.17.mixed, f32[128,2048]{1,0:T(8,128)} %get-tuple-element.22.combined, bf16[256,2048]{1,0:T(8,128)(2,1)} %get-tuple-element.23.a, ...), custom_call_target="tpu_custom_call" | custom-call | tf_op jit(solution)/shard_map/pallas_call | solution.py:672
  (1 shorter events, 0.0 us)
